TPU v7x, 256 devices: a whole 4x4x8 slice. The times are simulated.
256 devices in a mesh: seq: 128 (over x_lo, y, z, core), head: 2 (over x_hi).
Axes of the slice: x: 4 (x_hi: 2, x_lo: 2; x = x_hi * 2 + x_lo), y: 4, z: 8, core: 2. Of those that a mesh axis runs over, the one named last changes fastest.
Arguments:
- queries: bfloat16 [16384, 3072], P('seq', 'head'), may hold values from -6 to 6
- keys: bfloat16 [16384, 3072], P('seq', 'head'), may hold values from -6 to 6
- values: bfloat16 [16384, 3072], P('seq', 'head'), may hold values from -6 to 6
- cache_k: bfloat16 [2048, 3072], P('seq', 'head'), may hold values from -6 to 6
- cache_v: bfloat16 [2048, 3072], P('seq', 'head'), may hold values from -6 to 6
- sink_k: bfloat16 [8, 3072], P(None, 'head'), may hold values from -6 to 6
- sink_v: bfloat16 [8, 3072], P(None, 'head'), may hold values from -6 to 6
- suffix_lengths: int32 [32], replicated, may hold values from 1 to 1024, 16384 in all
- request_group: int32 [32], replicated, may hold values from 0 to 1
- w_out: bfloat16 [3072, 3072], P('head'), may hold values from -0.109375 to 0.109375
Outputs:
- projected: bfloat16 [3072, 16384], P('head', 'seq')
All inputs are finite; a program needn't handle non-finite values.
Results may differ from a plain program's by a relative error of at most 0.011.
Values may be sent and summed in bfloat16 or wider, within the bound.
No kernel may reach another device: no remote copies, remote signals or barrier semaphores. Data moves between devices by JAX's collectives and lax.ppermute only.
A program may use at most 128 MiB of HBM per device.

v0:
```python
import math

import jax
import jax.numpy as jnp
from jax import lax
from jax.sharding import PartitionSpec as P

HD = 96
W = 1024
SINKS = 4


def from_behind(array, axis, by):
    devices = lax.axis_size(axis)
    pairs = [(i, i + by) for i in range(devices) if 0 <= i + by < devices]
    return lax.ppermute(array, axis, pairs)


def describe(index, starts, lengths, groups):
    inside = (starts[None, :] <= index[:, None]) & (index[:, None] < (starts + lengths)[None, :])
    flag = inside.astype(jnp.int32)
    found = jnp.sum(flag, axis=1)
    request = jnp.sum(flag * jnp.arange(starts.shape[0], dtype=jnp.int32)[None, :], axis=1)
    request = jnp.where(found > 0, request, -1)
    offset = index - jnp.sum(flag * starts[None, :], axis=1)
    group = jnp.sum(flag * groups[None, :], axis=1)
    return (request, offset, group)


def shards(
    queries, keys, values, cache_k, cache_v, sink_k, sink_v, suffix_lengths, request_group, w_out
):
    rows, width = queries.shape
    heads = width // HD
    scale = 1.0 / math.sqrt(HD)
    device = lax.axis_index("seq")
    starts = jnp.cumsum(suffix_lengths) - suffix_lengths
    index = device * rows + jnp.arange(rows, dtype=jnp.int32)
    req_q, off_q, grp_q = describe(index, starts, suffix_lengths, request_group)
    q_three = queries.reshape(rows, heads, HD)

    def absorb(state, key_rows, value_rows, mask):
        top, den, acc = state
        count = key_rows.shape[0]
        k_three = key_rows.reshape(count, heads, HD)
        v_three = value_rows.reshape(count, heads, HD)
        score = (
            jnp.einsum("shd,khd->hsk", q_three, k_three, preferred_element_type=jnp.float32) * scale
        )
        score = jnp.where(mask[None], score, jnp.float32(-1e30))
        new_top = jnp.maximum(top, jnp.max(score, axis=2))
        factor = jnp.exp(top - new_top)
        prob = jnp.where(mask[None], jnp.exp(score - new_top[:, :, None]), jnp.float32(0.0))
        den = den * factor + jnp.sum(prob, axis=2)
        part = jnp.einsum(
            "hsk,khd->hsd", prob.astype(jnp.bfloat16), v_three, preferred_element_type=jnp.float32
        )
        acc = acc * factor[:, :, None] + part
        return (new_top, den, acc)

    def suffix_mask(near):
        req_k, off_k, grp_k = describe(near, starts, suffix_lengths, request_group)
        return (
            (req_k[None, :] == req_q[:, None])
            & (near[None, :] <= index[:, None])
            & (index[:, None] - near[None, :] < W)
            & (near[None, :] >= 0)
        )

    state = (
        jnp.full((heads, rows), -1e30, jnp.float32),
        jnp.zeros((heads, rows), jnp.float32),
        jnp.zeros((heads, rows, HD), jnp.float32),
    )
    sink_group = jnp.arange(sink_k.shape[0], dtype=jnp.int32) // SINKS
    state = absorb(state, sink_k, sink_v, grp_q[:, None] == sink_group[None, :])
    pieces = (
        lax.all_gather(cache_k, "seq", axis=0, tiled=True),
        lax.all_gather(cache_v, "seq", axis=0, tiled=True),
    )
    slot = jnp.arange(pieces[0].shape[0], dtype=jnp.int32)
    state = absorb(
        state,
        pieces[0],
        pieces[1],
        (grp_q[:, None] == (slot // W)[None, :]) & ((slot % W)[None, :] > off_q[:, None]),
    )
    state = absorb(state, keys, values, suffix_mask(index))
    reach = W // rows
    current = (keys, values)
    for step in range(1, reach + 1):
        current = from_behind((current[0], current[1]), "seq", 1)
        near = (device - step) * rows + jnp.arange(rows, dtype=jnp.int32)
        state = absorb(state, current[0], current[1], suffix_mask(near))
    top, den, acc = state
    attn = (acc / den[:, :, None]).transpose(1, 0, 2).reshape(rows, width).astype(jnp.bfloat16)
    return lax.psum_scatter(
        jnp.einsum("cd,sc->ds", w_out, attn, preferred_element_type=jnp.float32).astype(
            jnp.bfloat16
        ),
        "head",
        scatter_dimension=0,
        tiled=True,
    )


def solution(mesh):
    placed = (
        P("seq", "head"),
        P("seq", "head"),
        P("seq", "head"),
        P("seq", "head"),
        P("seq", "head"),
        P(None, "head"),
        P(None, "head"),
        P(),
        P(),
        P("head", None),
    )
    return jax.shard_map(
        shards, mesh=mesh, in_specs=placed, out_specs=P("head", "seq"), check_vma=False
    )
```

profile of v0, /device:TPU:9, one launch (start us, length us, event | category | flops | bytes accessed | tf_op | source)
XLA Modules:
  0.0 551.6 jit_solution(7046040993679264815)
XLA Ops:
  8.1 4.1 collective-permute-start
  17.9 3.9 collective-permute-start.2
  21.9 3.8 collective-permute-start.3
  29.2 2.6 collective-permute-start.4
  32.3 4.5 collective-permute-start.5
  38.1 1.9 copy.96
  44.4 2.2 collective-permute-start.7
  47.6 2.3 collective-permute-done.6
  49.9 4.4 collective-permute-start.8
  54.6 4.4 collective-permute-start.9
  65.8 3.9 collective-permute-start.11
  69.7 2.0 fusion.168
  77.4 3.0 fusion.167
  82.3 3.4 collective-permute-start.12
  85.7 4.4 collective-permute-start.13
  90.2 2.9 fusion.166
  98.8 2.9 fusion.165
  105.6 3.9 collective-permute-start.15
  109.6 3.0 fusion.164
  116.3 1.9 copy.117
  118.3 2.9 fusion.163
  125.1 3.0 fusion.162
  128.0 144.4 %all-gather.3.cloned.1.call-done = bf16[2048,1536]{1,0:T(8,128)(2,1)} async-done(((bf16[16,1536]{1,0:T(8,128)(2,1)}), bf16[2048,1536]{1,0:T(8,128)(2,1)}) %all-gather.3.cloned.1.call-update) | async-done | bytes 6291472 | tf_op jit(solution)/shard_map/all_gather | solution.py:78
  272.4 8.7 %copy.93 = bf16[2048,1536]{0,1:T(8,128)(2,1)} copy(bf16[2048,1536]{1,0:T(8,128)(2,1)} %all-gather.3.cloned.1.call-done) | data formatting | bytes 12582912 | tf_op jit(solution)/shard_map/all_gather | solution.py:78
  281.1 5.7 %fusion = (f32[16,128]{1,0:T(8,128)S(1)}, f32[16,128,2048]{2,1,0:T(8,128)S(1)}) fusion(pred[128,2048]{1,0:T(8,128)(4,1)} %compare_and_fusion, bf16[128,16,96]{0,2,1:T(8,128)(2,1)S(1)} %bitcast.301, bf16[2048,16,96]{0,2,1:T(8,128)(2,1)} %bitcast.302), kind=kOutput, calls=%fused_computation.2 | convolution fusion | flops 817887232 | bytes 23732224 | tf_op jit(solution)/shard_map/shd,khd->hsk/dot_general | solution.py:48
  288.3 4.4 copy-done
  292.7 5.6 %fusion.1 = f32[16,128]{1,0:T(8,128)} fusion(f32[16,128,2048]{2,1,0:T(8,128)S(1)} %get-tuple-element.97, f32[16,128]{1,0:T(8,128)S(1)} %get-tuple-element.62, pred[128,2048]{1,0:T(8,128)(4,1)S(1)} %copy-done.6), kind=kLoop, calls=%fused_computation.3 | loop fusion | flops 20969472 | bytes 17055744 | tf_op jit(solution)/shard_map/reduce_sum | solution.py:54
  298.2 190.1 %all-gather.5.cloned.1.call-done = bf16[2048,1536]{1,0:T(8,128)(2,1)} async-done(((bf16[16,1536]{1,0:T(8,128)(2,1)}), bf16[2048,1536]{1,0:T(8,128)(2,1)}) %all-gather.5.cloned.1.call-update) | async-done | bytes 6291472 | tf_op jit(solution)/shard_map/all_gather | solution.py:79
  488.4 8.7 %copy.94 = bf16[2048,1536]{0,1:T(8,128)(2,1)} copy(bf16[2048,1536]{1,0:T(8,128)(2,1)} %all-gather.5.cloned.1.call-done) | data formatting | bytes 12582912 | tf_op jit(solution)/shard_map/all_gather | solution.py:79
  497.4 10.3 %fusion.38 = f32[128,16,96]{0,2,1:T(8,128)S(1)} fusion(bf16[2048,16,96]{0,2,1:T(8,128)(2,1)} %bitcast.305, f32[16,128,2048]{2,1,0:T(8,128)} %copy-done, f32[16,128]{1,0:T(8,128)} %copy-done.55, pred[128,2048]{1,0:T(8,128)(4,1)S(1)} %copy-done.7), kind=kOutput, calls=%fused_computation.59 | convolution fusion | flops 826277888 | bytes 24125440 | tf_op jit(solution)/shard_map/hsk,khd->hsd/dot_general | solution.py:55
  516.1 2.3 fusion.6
  518.5 24.7 %reduce-scatter.2.cloned.1.call-done = bf16[1536,128]{0,1:T(8,128)(2,1)} async-done(((bf16[3072,128]{0,1:T(8,128)(2,1)}), bf16[1536,128]{0,1:T(8,128)(2,1)}) %reduce-scatter.2.cloned.1.call-update) | async-done | bytes 393232 | tf_op jit(solution)/shard_map/reduce_scatter | solution.py:97
  (224 shorter events, 61.0 us)
Async XLA Ops:
  6.5 265.9 %all-gather.3.cloned.1.call-start = ((), (), s32[]{:S(2)}) async-start(), calls=%async_computation.1 | async-start | bytes 6340608 | tf_op jit(solution)/shard_map/all_gather | solution.py:78
  7.3 481.1 %all-gather.5.cloned.1.call-start = ((), (), s32[]{:S(2)}) async-start(), calls=%async_computation.2 | async-start | bytes 6340608 | tf_op jit(solution)/shard_map/all_gather | solution.py:79
  8.0 535.1 %reduce-scatter.2.cloned.1.call-start = ((), (), s32[]{:S(2)}) async-start(), calls=%async_computation.3 | async-start | bytes 1179648 | tf_op jit(solution)/shard_map/reduce_scatter | solution.py:97
  8.1 9.8 %collective-permute-start = (bf16[128,1536]{1,0:T(8,128)(2,1)}, bf16[128,1536]{1,0:T(8,128)(2,1)S(1)}, u32[]{:S(2)}, u32[]{:S(2)}) collective-permute-start(bf16[128,1536]{1,0:T(8,128)(2,1)} %param.11), channel_id=1, source_target_pairs={{0,2},{2,4},{4,6},{6,8},{8,10},{10,12},{12,14},{14,16},{16,18},{18... | collective-permute-start | bytes 1179656 | tf_op jit(solution)/shard_map/ppermute | solution.py:16
  12.2 9.7 %collective-permute-start.1 = (bf16[128,1536]{1,0:T(8,128)(2,1)}, bf16[128,1536]{1,0:T(8,128)(2,1)S(1)}, u32[]{:S(2)}, u32[]{:S(2)}) collective-permute-start(bf16[128,1536]{1,0:T(8,128)(2,1)} %param.12), channel_id=1, source_target_pairs={{0,2},{2,4},{4,6},{6,8},{8,10},{10,12},{12,14},{14,16},{16,18},{18... | collective-permute-start | bytes 1179656 | tf_op jit(solution)/shard_map/ppermute | solution.py:16
  16.7 42.3 %copy-start.57 = (pred[128,8]{0,1:T(8,128)(4,1)}, pred[128,8]{0,1:T(8,128)(4,1)S(1)}, u32[]{:S(2)}) copy-start(pred[128,8]{0,1:T(8,128)(4,1)S(1)} %broadcast_compare_fusion) | copy-start | bytes 3076
  17.9 41.1 %copy-start.27 = (pred[128,128]{0,1:T(8,128)(4,1)}, pred[128,128]{0,1:T(8,128)(4,1)S(1)}, u32[]{:S(2)}) copy-start(pred[128,128]{0,1:T(8,128)(4,1)S(1)} %get-tuple-element.69) | copy-start | bytes 49156
  17.9 11.3 %collective-permute-start.2 = (bf16[128,1536]{1,0:T(8,128)(2,1)S(1)}, bf16[128,1536]{1,0:T(8,128)(2,1)}, u32[]{:S(2)}, u32[]{:S(2)}) collective-permute-start(bf16[128,1536]{1,0:T(8,128)(2,1)S(1)} %collective-permute-done), channel_id=1, source_target_pairs={{0,2},{2,4},{4,6},{6,8},{8,10},{10,12},{12,14},{14,16},{16,18},{18... | collective-permute-start | bytes 1179656 | tf_op jit(solution)/shard_map/ppermute | solution.py:16
  21.9 10.5 %collective-permute-start.3 = (bf16[128,1536]{1,0:T(8,128)(2,1)S(1)}, bf16[128,1536]{1,0:T(8,128)(2,1)S(1)}, u32[]{:S(2)}, u32[]{:S(2)}) collective-permute-start(bf16[128,1536]{1,0:T(8,128)(2,1)S(1)} %collective-permute-done.1), channel_id=1, source_target_pairs={{0,2},{2,4},{4,6},{6,8},{8,10},{10,12},{12,14},{14,16},{16,18},{18... | collective-permute-start | bytes 1179656 | tf_op jit(solution)/shard_map/ppermute | solution.py:16
  29.2 13.3 %collective-permute-start.4 = (bf16[128,1536]{1,0:T(8,128)(2,1)}, bf16[128,1536]{1,0:T(8,128)(2,1)}, u32[]{:S(2)}, u32[]{:S(2)}) collective-permute-start(bf16[128,1536]{1,0:T(8,128)(2,1)} %collective-permute-done.2), channel_id=1, source_target_pairs={{0,2},{2,4},{4,6},{6,8},{8,10},{10,12},{12,14},{14,16},{16,18},{18... | collective-permute-start | bytes 1179656 | tf_op jit(solution)/shard_map/ppermute | solution.py:16
  32.3 26.7 %copy-start.19 = (bf16[128,1536]{1,0:T(8,128)(2,1)}, bf16[128,1536]{1,0:T(8,128)(2,1)S(1)}, u32[]{:S(2)}) copy-start(bf16[128,1536]{1,0:T(8,128)(2,1)S(1)} %collective-permute-done.3) | copy-start | bytes 1179652
  32.3 12.0 %collective-permute-start.5 = (bf16[128,1536]{1,0:T(8,128)(2,1)S(1)}, bf16[128,1536]{1,0:T(8,128)(2,1)}, u32[]{:S(2)}, u32[]{:S(2)}) collective-permute-start(bf16[128,1536]{1,0:T(8,128)(2,1)S(1)} %collective-permute-done.3), channel_id=1, source_target_pairs={{0,2},{2,4},{4,6},{6,8},{8,10},{10,12},{12,14},{14,16},{16,18},{18... | collective-permute-start | bytes 1179656 | tf_op jit(solution)/shard_map/ppermute | solution.py:16
  42.5 7.4 %collective-permute-start.6 = (bf16[128,1536]{1,0:T(8,128)(2,1)}, bf16[128,1536]{1,0:T(8,128)(2,1)}, u32[]{:S(2)}, u32[]{:S(2)}) collective-permute-start(bf16[128,1536]{1,0:T(8,128)(2,1)} %collective-permute-done.4), channel_id=1, source_target_pairs={{0,2},{2,4},{4,6},{6,8},{8,10},{10,12},{12,14},{14,16},{16,18},{18... | collective-permute-start | bytes 1179656 | tf_op jit(solution)/shard_map/ppermute | solution.py:16
  44.4 10.2 %collective-permute-start.7 = (bf16[128,1536]{1,0:T(8,128)(2,1)}, bf16[128,1536]{1,0:T(8,128)(2,1)}, u32[]{:S(2)}, u32[]{:S(2)}) collective-permute-start(bf16[128,1536]{1,0:T(8,128)(2,1)} %collective-permute-done.5), channel_id=1, source_target_pairs={{0,2},{2,4},{4,6},{6,8},{8,10},{10,12},{12,14},{14,16},{16,18},{18... | collective-permute-start | bytes 1179656 | tf_op jit(solution)/shard_map/ppermute | solution.py:16
  49.9 14.0 %collective-permute-start.8 = (bf16[128,1536]{1,0:T(8,128)(2,1)}, bf16[128,1536]{1,0:T(8,128)(2,1)}, u32[]{:S(2)}, u32[]{:S(2)}) collective-permute-start(bf16[128,1536]{1,0:T(8,128)(2,1)} %collective-permute-done.6), channel_id=1, source_target_pairs={{0,2},{2,4},{4,6},{6,8},{8,10},{10,12},{12,14},{14,16},{16,18},{18... | collective-permute-start | bytes 1179656 | tf_op jit(solution)/shard_map/ppermute | solution.py:16
  54.6 11.2 %collective-permute-start.9 = (bf16[128,1536]{1,0:T(8,128)(2,1)}, bf16[128,1536]{1,0:T(8,128)(2,1)}, u32[]{:S(2)}, u32[]{:S(2)}) collective-permute-start(bf16[128,1536]{1,0:T(8,128)(2,1)} %collective-permute-done.7), channel_id=1, source_target_pairs={{0,2},{2,4},{4,6},{6,8},{8,10},{10,12},{12,14},{14,16},{16,18},{18... | collective-permute-start | bytes 1179656 | tf_op jit(solution)/shard_map/ppermute | solution.py:16
  63.9 18.4 %collective-permute-start.10 = (bf16[128,1536]{1,0:T(8,128)(2,1)}, bf16[128,1536]{1,0:T(8,128)(2,1)}, u32[]{:S(2)}, u32[]{:S(2)}) collective-permute-start(bf16[128,1536]{1,0:T(8,128)(2,1)} %collective-permute-done.8), channel_id=1, source_target_pairs={{0,2},{2,4},{4,6},{6,8},{8,10},{10,12},{12,14},{14,16},{16,18},{18... | collective-permute-start | bytes 1179656 | tf_op jit(solution)/shard_map/ppermute | solution.py:16
  65.8 19.9 %collective-permute-start.11 = (bf16[128,1536]{1,0:T(8,128)(2,1)}, bf16[128,1536]{1,0:T(8,128)(2,1)}, u32[]{:S(2)}, u32[]{:S(2)}) collective-permute-start(bf16[128,1536]{1,0:T(8,128)(2,1)} %collective-permute-done.9), channel_id=1, source_target_pairs={{0,2},{2,4},{4,6},{6,8},{8,10},{10,12},{12,14},{14,16},{16,18},{18... | collective-permute-start | bytes 1179656 | tf_op jit(solution)/shard_map/ppermute | solution.py:16
  82.3 21.4 %collective-permute-start.12 = (bf16[128,1536]{1,0:T(8,128)(2,1)}, bf16[128,1536]{1,0:T(8,128)(2,1)}, u32[]{:S(2)}, u32[]{:S(2)}) collective-permute-start(bf16[128,1536]{1,0:T(8,128)(2,1)} %collective-permute-done.10), channel_id=1, source_target_pairs={{0,2},{2,4},{4,6},{6,8},{8,10},{10,12},{12,14},{14,16},{16,18},{18... | collective-permute-start | bytes 1179656 | tf_op jit(solution)/shard_map/ppermute | solution.py:16
  85.7 19.9 %collective-permute-start.13 = (bf16[128,1536]{1,0:T(8,128)(2,1)}, bf16[128,1536]{1,0:T(8,128)(2,1)}, u32[]{:S(2)}, u32[]{:S(2)}) collective-permute-start(bf16[128,1536]{1,0:T(8,128)(2,1)} %collective-permute-done.11), channel_id=1, source_target_pairs={{0,2},{2,4},{4,6},{6,8},{8,10},{10,12},{12,14},{14,16},{16,18},{18... | collective-permute-start | bytes 1179656 | tf_op jit(solution)/shard_map/ppermute | solution.py:16
  103.7 17.5 %collective-permute-start.14 = (bf16[128,1536]{1,0:T(8,128)(2,1)}, bf16[128,1536]{1,0:T(8,128)(2,1)}, u32[]{:S(2)}, u32[]{:S(2)}) collective-permute-start(bf16[128,1536]{1,0:T(8,128)(2,1)} %collective-permute-done.12), channel_id=1, source_target_pairs={{0,2},{2,4},{4,6},{6,8},{8,10},{10,12},{12,14},{14,16},{16,18},{18... | collective-permute-start | bytes 1179656 | tf_op jit(solution)/shard_map/ppermute | solution.py:16
  105.6 17.5 %collective-permute-start.15 = (bf16[128,1536]{1,0:T(8,128)(2,1)}, bf16[128,1536]{1,0:T(8,128)(2,1)}, u32[]{:S(2)}, u32[]{:S(2)}) collective-permute-start(bf16[128,1536]{1,0:T(8,128)(2,1)} %collective-permute-done.13), channel_id=1, source_target_pairs={{0,2},{2,4},{4,6},{6,8},{8,10},{10,12},{12,14},{14,16},{16,18},{18... | collective-permute-start | bytes 1179656 | tf_op jit(solution)/shard_map/ppermute | solution.py:16
  286.9 210.2 %copy-start.7 = (pred[128,2048]{1,0:T(8,128)(4,1)S(1)}, pred[128,2048]{1,0:T(8,128)(4,1)}, u32[]{:S(2)}) copy-start(pred[128,2048]{1,0:T(8,128)(4,1)} %compare_and_fusion) | copy-start | bytes 786436
  288.3 208.8 %copy-start.55 = (f32[16,128]{1,0:T(8,128)}, f32[16,128]{1,0:T(8,128)S(1)}, u32[]{:S(2)}) copy-start(f32[16,128]{1,0:T(8,128)S(1)} %get-tuple-element.62) | copy-start | bytes 24580
  497.3 13.5 %copy-start.31 = (f32[16,128]{1,0:T(8,128)S(1)}, f32[16,128]{1,0:T(8,128)}, u32[]{:S(2)}) copy-start(f32[16,128]{1,0:T(8,128)} %get-tuple-element.98) | copy-start | bytes 24580
  497.3 13.5 %copy-start.33 = (f32[16,128]{1,0:T(8,128)S(1)}, f32[16,128]{1,0:T(8,128)}, u32[]{:S(2)}) copy-start(f32[16,128]{1,0:T(8,128)} %get-tuple-element.92) | copy-start | bytes 24580
  497.3 13.5 %copy-start.35 = (f32[16,128]{1,0:T(8,128)S(1)}, f32[16,128]{1,0:T(8,128)}, u32[]{:S(2)}) copy-start(f32[16,128]{1,0:T(8,128)} %get-tuple-element.88) | copy-start | bytes 24580
  497.3 13.5 %copy-start.37 = (f32[16,128]{1,0:T(8,128)S(1)}, f32[16,128]{1,0:T(8,128)}, u32[]{:S(2)}) copy-start(f32[16,128]{1,0:T(8,128)} %copy-done.36) | copy-start | bytes 24580
  497.3 13.5 %copy-start.49 = (f32[16,128]{1,0:T(8,128)S(1)}, f32[16,128]{1,0:T(8,128)}, u32[]{:S(2)}) copy-start(f32[16,128]{1,0:T(8,128)} %get-tuple-element.84) | copy-start | bytes 24580
  497.3 14.3 %copy-start.38 = (bf16[8,16,96]{2,1,0:T(8,128)(2,1)S(1)}, bf16[8,16,96]{2,1,0:T(8,128)(2,1)}, u32[]{:S(2)}) copy-start(bf16[8,16,96]{2,1,0:T(8,128)(2,1)} %reshape.1640) | copy-start | bytes 73732
  497.4 15.4 %copy-start.9 = (bf16[128,1536]{0,1:T(8,128)(2,1)S(1)}, bf16[128,1536]{0,1:T(8,128)(2,1)}, u32[]{:S(2)}) copy-start(bf16[128,1536]{0,1:T(8,128)(2,1)} %copy.96) | copy-start | bytes 1179652
  497.4 15.7 %copy-start.10 = (bf16[128,1536]{0,1:T(8,128)(2,1)S(1)}, bf16[128,1536]{0,1:T(8,128)(2,1)}, u32[]{:S(2)}) copy-start(bf16[128,1536]{0,1:T(8,128)(2,1)} %copy.99) | copy-start | bytes 1179652
  (48 other events, 421.2 us)
Sparse Core Ops, SparseCore 0:
  9.2 263.1 all-gather.2
  274.3 214.0 all-gather.4
  518.6 24.5 reduce-scatter.1
where the time goes:
time: 554 us; the launch traced here: 552 us
  waiting for transfers between devices  364 us (66%)
  local copies, waits for them, and re-layouts  59.7 us (11%)
  starting transfers between devices  53.3 us (10%)
  matrix products  45.1 us (8%)
  other arithmetic  15.2 us (3%)
  between operations  14.4 us (3%)
    all_gather x1, waiting for transfers between devices, shards(): lax.all_gather(cache_v, 'seq', axis=0, tiled=True)  190 us
    all_gather x1, waiting for transfers between devices, shards(): lax.all_gather(cache_k, 'seq', axis=0, tiled=True)  144 us
    ppermute x16, starting transfers between devices, from_behind(): return lax.ppermute(array, axis, pairs)  53.2 us
    dot_general x11, matrix products, absorb(): jnp.einsum('shd,khd->hsk', q_three, k_three, preferred_element_type=jnp.f...  28.7 us
    ppermute x16, local copies, waits for them, and re-layouts, from_behind(): return lax.ppermute(array, axis, pairs)  28 us
    reduce_scatter x1, waiting for transfers between devices, shards(): lax.psum_scatter(jnp.einsum('cd,sc->ds', w_out, attn, preferred_element_t...  24.7 us
    dot_general x11, matrix products, absorb(): jnp.einsum('hsk,khd->hsd', prob.astype(jnp.bfloat16), v_three, preferred_...  14.1 us
  transfers between devices with their start and end apart: 19, of which 6 were waited for; matrix products, arithmetic and copies ran while one was open for 15% of the time, Pallas kernels for 0%

commit v1 on v0

v1 whole, which is shorter than its diff:
```python
import functools
import math

import jax
import jax.numpy as jnp
from jax import lax
from jax.experimental import pallas as pl
from jax.experimental.pallas import tpu as pltpu
from jax.sharding import PartitionSpec as P

HD = 96
W = 1024
SINKS = 4
G = 2
RING = 16
BLK = 128
QB = 256
CH = 256
LANES = 128
FAR = 1 << 28
LOW = -1e30


def pack_kernel(head, q_ref, k_ref, v_ref, ck_ref, cv_ref, sk_ref, sv_ref, out_ref, sink_ref):
    heads = q_ref.shape[1] // HD
    for which, ref in enumerate((q_ref, k_ref, v_ref)):
        turned = ref[...].T
        for p in range(heads):
            out_ref[p, which * HD : (which + 1) * HD, :] = turned[p * HD : (p + 1) * HD, :]
    rows = ck_ref.shape[0]
    fill = jnp.zeros((rows, LANES - HD), ck_ref.dtype)
    for which, ref in enumerate((ck_ref, cv_ref)):
        for p in range(heads):
            piece = jnp.concatenate([ref[:, p * HD : (p + 1) * HD], fill], axis=1)
            base = 3 * HD + which * rows
            out_ref[p, base : base + rows, :] = piece
    width = sk_ref.shape[1]
    column = lax.broadcasted_iota(jnp.int32, (width, LANES), 0)
    lane = lax.broadcasted_iota(jnp.int32, (width, LANES), 1)
    pick = ((column == head[0] * HD + lane) & (lane < HD)).astype(jnp.float32).astype(jnp.bfloat16)
    for which, ref in enumerate((sk_ref, sv_ref)):
        piece = jnp.dot(ref[...], pick, preferred_element_type=jnp.float32)
        piece = jnp.concatenate([piece, jnp.zeros_like(piece)], axis=0)
        sink_ref[which * 16 : (which + 1) * 16, :] = piece.astype(jnp.bfloat16)


def attend_kernel(
    place, lengths, groups, sink_ref, own_ref, win_ref, *rest, rings
):
    caches = rest[: rings]
    out_ref, key_ref, val_ref, low_ref, need = rest[rings:]
    ring = place[0]
    base = ring * RING * BLK
    front = W
    own = RING * BLK
    cache_at = front + own
    blocks = own // QB
    factor = (1.0 / math.sqrt(HD)) * math.log2(math.e)
    pad = jnp.zeros((LANES - HD, BLK), jnp.bfloat16)

    def turn(piece):
        return jnp.concatenate([piece, pad], axis=0).T

    for j in range(RING // 2):
        key_ref[j * BLK : (j + 1) * BLK, :] = turn(win_ref[j, 0:HD, :])
        val_ref[j] = win_ref[j, HD : 2 * HD, :]
    for j in range(RING):
        at = front + j * BLK
        key_ref[at : at + BLK, :] = turn(own_ref[j, HD : 2 * HD, :])
        val_ref[front // BLK + j] = own_ref[j, 2 * HD : 3 * HD, :]
    rows = RING * 16
    for k in range(rings):
        x_lo = (ring // 4 + k // 4) % 2
        y = (ring % 4 + k % 4) % 4
        source = lax.rem(lax.rem(ring, 4) + 4 - k % 4, 4) + 4 * lax.rem(ring // 4 + k // 4, 2)
        piece = caches[k][...]
        keys = piece[:, 0:16, :].reshape(rows, LANES)
        vals = piece[:, 16:32, :].reshape(rows, LANES)
        at = pl.multiple_of(cache_at + source * rows, rows)
        key_ref[pl.ds(at, rows), :] = keys
        turned = vals.T
        for half in range(rows // BLK):
            val_ref[cache_at // BLK + source * (rows // BLK) + half] = turned[
                0:HD, half * BLK : (half + 1) * BLK
            ]

    for b in range(blocks):
        need[b] = FAR
        need[blocks + b] = FAR
        need[2 * blocks + b] = FAR

    def one_request(r, carry):
        start, start_col, group_col = carry
        length = lengths[r]
        group = groups[r]
        first = jnp.maximum((start - base) // QB, 0)
        last = jnp.minimum((start + length - 1 - base) // QB, blocks - 1)
        first = jnp.where(start < base, 0, first)

        def mark(b, _):
            need[b] = jnp.minimum(need[b], start)
            offset = jnp.maximum(base + b * QB - start, 0)
            at = (1 + group) * blocks + b
            need[at] = jnp.minimum(need[at], offset)
            return 0

        @pl.when((start < base + own) & (start + length > base))
        def _():
            lax.fori_loop(first, last + 1, mark, 0)

        row = lax.broadcasted_iota(jnp.int32, start_col.shape, 0)
        start_col = jnp.where(row == r, start, start_col)
        group_col = jnp.where(row == r, group, group_col)
        return (start + length, start_col, group_col)

    reqs = lengths.shape[0]
    column = jnp.zeros((reqs, QB), jnp.int32)
    _, start_col, group_col = lax.fori_loop(0, reqs, one_request, (jnp.int32(0), column, column))

    lane = lax.broadcasted_iota(jnp.int32, (1, QB), 1)
    row_iota = lax.broadcasted_iota(jnp.int32, (CH, QB), 0)
    sink_row = lax.broadcasted_iota(jnp.int32, (16, QB), 0)

    def dot(a, b):
        return jnp.dot(a, b, preferred_element_type=jnp.float32)

    def one_block(b, _):
        index = base + b * QB + lane
        begun = start_col <= index
        start_q = jnp.max(jnp.where(begun, start_col, 0), axis=0, keepdims=True)
        here = begun & (start_col == start_q)
        group_q = jnp.max(jnp.where(here, group_col, 0), axis=0, keepdims=True)
        offset = index - start_q
        low_suffix = jnp.maximum(start_q, index - (W - 1)) - base + front
        low_ref[0] = jnp.broadcast_to(low_suffix, (8, QB))
        for g in range(G):
            low_g = jnp.where(group_q == g, cache_at + g * W + offset + 1, FAR)
            low_ref[1 + g] = jnp.broadcast_to(low_g, (8, QB))
        low_ref[1 + G] = jnp.full((8, QB), FAR, jnp.int32)
        q_t = jnp.concatenate([own_ref[2 * b, 0:HD, :], own_ref[2 * b + 1, 0:HD, :]], axis=1)
        q_t = jnp.concatenate([q_t, jnp.zeros((LANES - HD, QB), jnp.bfloat16)], axis=0)

        def values(at):
            slot = at // BLK
            return jnp.concatenate([val_ref[slot], val_ref[slot + 1]], axis=1)

        at0 = pl.multiple_of(front + b * QB, CH)
        s_d = dot(key_ref[pl.ds(at0, CH), :], q_t)
        key_at = row_iota + at0
        s_d = jnp.where((key_at >= low_suffix) & (key_at <= at0 + lane), s_d, LOW)
        s_s = dot(sink_ref[0:16, :], q_t)
        s_s = jnp.where((sink_row // SINKS == group_q) & (sink_row < G * SINKS), s_s, LOW)
        top = jnp.maximum(jnp.max(s_d, axis=0, keepdims=True), jnp.max(s_s, axis=0, keepdims=True))
        p_d = jnp.exp2((s_d - top) * factor)
        p_s = jnp.exp2((s_s - top) * factor)
        den = jnp.sum(p_d, axis=0, keepdims=True) + jnp.sum(p_s, axis=0, keepdims=True)
        sink_v = sink_ref[16:32, :].T[0:HD, :]
        acc = dot(values(at0), p_d.astype(jnp.bfloat16)) + dot(sink_v, p_s.astype(jnp.bfloat16))

        first = jnp.maximum(need[b], base + b * QB - (W - 1)) - base + front
        n_suffix = front // CH + b - first // CH
        c0 = [jnp.minimum((need[(1 + g) * blocks + b] + 1) // CH, W // CH) for g in range(G)]
        n0, n1 = [W // CH - c for c in c0]
        total = n_suffix + n0 + n1

        def where_is(j):
            in0 = j - n_suffix
            in1 = in0 - n0
            at = jnp.where(
                in0 < 0,
                (first // CH + j) * CH,
                jnp.where(
                    in1 < 0,
                    cache_at + (c0[0] + in0) * CH,
                    jnp.where(j < total, cache_at + W + (c0[1] + in1) * CH, 0),
                ),
            )
            kind = jnp.where(in0 < 0, 0, jnp.where(in1 < 0, 1, jnp.where(j < total, 2, 3)))
            return pl.multiple_of(at, CH), kind

        def step(j, state):
            top, den, acc = state
            scores, ats = [], []
            for u in range(2):
                at, kind = where_is(2 * j + u)
                s = dot(key_ref[pl.ds(at, CH), :], q_t)
                low = low_ref[kind][0:1, :]
                scores.append(jnp.where(row_iota + at >= low, s, LOW))
                ats.append(at)
            new = jnp.maximum(
                jnp.max(scores[0], axis=0, keepdims=True), jnp.max(scores[1], axis=0, keepdims=True)
            )
            new = jnp.maximum(top, new)
            fade = jnp.exp2((top - new) * factor)
            den = den * fade
            acc = acc * fade
            for u in range(2):
                p = jnp.exp2((scores[u] - new) * factor)
                den = den + jnp.sum(p, axis=0, keepdims=True)
                acc = acc + dot(values(ats[u]), p.astype(jnp.bfloat16))
            return (new, den, acc)

        top, den, acc = lax.fori_loop(0, (total + 1) // 2, step, (top, den, acc))
        done = (acc / den).astype(jnp.bfloat16)
        out_ref[2 * b] = done[:, 0:BLK]
        out_ref[2 * b + 1] = done[:, BLK:QB]
        return 0

    lax.fori_loop(0, blocks, one_block, 0)


def vmem():
    return pl.BlockSpec(memory_space=pltpu.VMEM)


def smem():
    return pl.BlockSpec(memory_space=pltpu.SMEM)


def shards(
    queries, keys, values, cache_k, cache_v, sink_k, sink_v, suffix_lengths, request_group, w_out
):
    rows, width = queries.shape
    heads = width // HD
    seq = lax.axis_size("seq")
    rings = seq // RING
    device = lax.axis_index("seq")
    half = lax.axis_index("head")
    chunk = 3 * HD + 32
    packed, sinks = pl.pallas_call(
        pack_kernel,
        out_shape=(
            jax.ShapeDtypeStruct((heads, chunk, LANES), jnp.bfloat16),
            jax.ShapeDtypeStruct((32, LANES), jnp.bfloat16),
        ),
        in_specs=[smem()] + [vmem()] * 7,
        out_specs=(vmem(), vmem()),
        name="pack",
    )(
        (device % RING).reshape(1), queries, keys, values, cache_k, cache_v, sink_k, sink_v
    )
    members = [[r * RING + i for i in range(RING)] for r in range(rings)]
    mine = lax.all_to_all(packed, "seq", 0, 0, axis_index_groups=members, tiled=True)
    cache = mine[:, 3 * HD :, :]

    def ring_after(r, k):
        return (r % 4 + k % 4) % 4 + 4 * ((r // 4 + k // 4) % 2)

    caches = [cache]
    for k in range(1, rings):
        pairs = [
            (r * RING + i, ring_after(r, k) * RING + i) for r in range(rings) for i in range(RING)
        ]
        caches.append(lax.ppermute(cache, "seq", pairs))
    window = lax.ppermute(
        mine[RING // 2 :, HD : 3 * HD, :], "seq", [(s, s + RING) for s in range(seq - RING)]
    )
    attn = pl.pallas_call(
        functools.partial(attend_kernel, rings=rings),
        out_shape=jax.ShapeDtypeStruct((RING, HD, BLK), jnp.bfloat16),
        in_specs=[smem()] * 3 + [vmem()] * (3 + rings),
        out_specs=vmem(),
        scratch_shapes=[
            pltpu.VMEM((W + RING * BLK + G * W, LANES), jnp.bfloat16),
            pltpu.VMEM(((W + RING * BLK + G * W) // BLK, HD, BLK), jnp.bfloat16),
            pltpu.VMEM((2 + G, 8, QB), jnp.int32),
            pltpu.SMEM((3 * RING * BLK // QB,), jnp.int32),
        ],
        name="attend",
    )((device // RING).reshape(1), suffix_lengths, request_group, sinks, mine, window, *caches)
    back = lax.all_to_all(attn, "seq", 0, 0, axis_index_groups=members, tiled=True)
    attn_t = back.reshape(width, rows)
    full = jnp.einsum("cd,cs->ds", w_out, attn_t, preferred_element_type=jnp.float32)
    features = full.shape[0] // 2
    keep = lax.dynamic_slice_in_dim(full, half * features, features, 0)
    give = lax.dynamic_slice_in_dim(full, (1 - half) * features, features, 0)
    got = lax.ppermute(give.astype(jnp.bfloat16), "head", [(0, 1), (1, 0)])
    return (keep + got.astype(jnp.float32)).astype(jnp.bfloat16)


def solution(mesh):
    placed = (
        P("seq", "head"),
        P("seq", "head"),
        P("seq", "head"),
        P("seq", "head"),
        P("seq", "head"),
        P(None, "head"),
        P(None, "head"),
        P(),
        P(),
        P("head", None),
    )
    return jax.shard_map(
        shards, mesh=mesh, in_specs=placed, out_specs=P("head", "seq"), check_vma=False
    )
```

time: 554 us -> 136 us (0.25)
  waiting for transfers between devices: 364 us -> 38.5 us
  local copies, waits for them, and re-layouts: 59.7 us -> 1.75 us
  blocking collectives: 0 us -> 43.2 us
  matrix products: 45.1 us -> 5.09 us
  starting transfers between devices: 53.3 us -> 22.6 us
  Pallas kernels: 0 us -> 24.6 us
  other arithmetic: 15.2 us -> 0.08 us
  between operations: 14.4 us -> 0.13 us
    all_gather x2 -> x0, waiting for transfers between devices: 335 us -> none  [the longest x1 190 us: shards(): lax.all_gather(cache_v, 'seq', axis=0, tiled=True)]
    all_to_all x0 -> x1, blocking collectives: none -> 43.2 us  [shards(): lax.all_to_all(packed, 'seq', 0, 0, axis_index_groups=members, tiled=True)]
    dot_general x23 -> x1, matrix products: 45.1 us -> 5.09 us  [shards(): jnp.einsum('cd,cs->ds', w_out, attn_t, preferred_element_type=jnp.float32)]
    ppermute x16 -> x9, starting transfers between devices: 53.2 us -> 16.9 us  [the longest x7 10.9 us: shards(): caches.append(lax.ppermute(cache, 'seq', pairs))]
    ppermute x16 -> x0, local copies, waits for them, and re-layouts: 28 us -> none  [from_behind(): return lax.ppermute(array, axis, pairs)]
    reduce_scatter x1 -> x0, waiting for transfers between devices: 24.7 us -> none  [shards(): lax.psum_scatter(jnp.einsum('cd,sc->ds', w_out, attn, preferred_element_t...]
    pallas_call x0 -> x2, Pallas kernels: none -> 24.6 us  [the longest x1 21.8 us: shards(): pl.pallas_call(functools.partial(attend_kernel, rings=rings), out_shape=j...]
    ppermute x16 -> x9, waiting for transfers between devices: 3.19 us -> 24 us  [the longest x7 14.7 us: shards(): caches.append(lax.ppermute(cache, 'seq', pairs))]
  transfers between devices with their start and end apart: 19 -> 10, of which waited for: 6 -> 5; matrix products, arithmetic and copies ran while one was open for 15% -> 0% of each run, Pallas kernels for 0% -> 0%
where the time goes in v1:
time: 136 us
  blocking collectives  43.2 us (32%)
  waiting for transfers between devices  38.5 us (28%)
  Pallas kernels  24.6 us (18%)
  starting transfers between devices  22.6 us (17%)
  matrix products  5.09 us (4%)
  local copies, waits for them, and re-layouts  1.75 us (1%)
    all_to_all x1, blocking collectives, shards(): lax.all_to_all(packed, 'seq', 0, 0, axis_index_groups=members, tiled=True)  43.2 us
    pallas_call x1, Pallas kernels, shards(): pl.pallas_call(functools.partial(attend_kernel, rings=rings), out_shape=j...  21.8 us
    ppermute x7, waiting for transfers between devices, shards(): caches.append(lax.ppermute(cache, 'seq', pairs))  14.7 us
    all_to_all x1, waiting for transfers between devices, shards(): lax.all_to_all(attn, 'seq', 0, 0, axis_index_groups=members, tiled=True)  14.5 us
    ppermute x7, starting transfers between devices, shards(): caches.append(lax.ppermute(cache, 'seq', pairs))  10.9 us
    ppermute x1, waiting for transfers between devices, shards(): got = lax.ppermute(give.astype(jnp.bfloat16), 'head', [(0, 1), (1, 0)])  9.27 us
    all_to_all x1, starting transfers between devices, shards(): lax.all_to_all(attn, 'seq', 0, 0, axis_index_groups=members, tiled=True)  5.68 us
    dot_general x1, matrix products, shards(): jnp.einsum('cd,cs->ds', w_out, attn_t, preferred_element_type=jnp.float32)  5.09 us
  transfers between devices with their start and end apart: 10, of which 5 were waited for; matrix products, arithmetic and copies ran while one was open for 0% of the time, Pallas kernels for 0%

profile of v1, /device:TPU:9, one launch (start us, length us, event | category | flops | bytes accessed | tf_op | source)
XLA Modules:
  0.0 136.0 jit_solution(15781550201506152573)
XLA Ops:
  0.0 2.8 %pack.1 = (bf16[16,320,128]{2,1,0:T(8,128)(2,1)}, bf16[32,128]{1,0:T(8,128)(2,1)}) custom-call(s32[1]{0:T(128)} %bitcast.1.head, bf16[128,1536]{1,0:T(8,128)(2,1)} %q_ref.1, bf16[128,1536]{1,0:T(8,128)(2,1)} %k_ref.1, bf16[128,1536]{1,0:T(8,128)(2,1)} %v_ref.1, bf16[16,1536]{1,0:T(8,128)(2,1)} %ck_ref.1, bf16[16,1536]{1,0:T(8,128)(2,1)} %cv_ref.1, ...), custom_call_target="tpu_custom_call" | custom-call | tf_op jit(solution)/shard_map/pack/pallas_call | solution.py:230
  2.8 43.2 %all_to_all.10.own_ref = bf16[16,320,128]{2,1,0:T(8,128)(2,1)S(1)} all-to-all(bf16[16,320,128]{2,1,0:T(8,128)(2,1)} %get-tuple-element.8), channel_id=1, replica_groups={{0,2,4,6,8,10,12,14,16,18,20,22,24,26,28,30},{32,34,36,38,40,42,44,46,4..., dimensions={0} | all-to-all | bytes 2621440 | tf_op jit(solution)/shard_map/all_to_all | solution.py:243
  46.1 3.2 %collective-permute-start = (bf16[8,192,128]{2,1,0:T(8,128)(2,1)S(1)}, bf16[8,192,128]{2,1,0:T(8,128)(2,1)S(1)}, u32[]{:S(2)}, u32[]{:S(2)}) collective-permute-start(bf16[8,192,128]{2,1,0:T(8,128)(2,1)S(1)} %slice.8), channel_id=1, source_target_pairs={{0,32},{2,34},{4,36},{6,38},{8,40},{10,42},{12,44},{14,46},{16,48}... | collective-permute-start | bytes 1179656 | tf_op jit(solution)/shard_map/ppermute | solution.py:255
  49.3 0.0 copy-start.1
  49.3 1.1 collective-permute-start.1
  50.4 1.0 collective-permute-start.2
  51.3 1.7 %collective-permute-start.3 = (bf16[16,32,128]{2,1,0:T(8,128)(2,1)S(1)}, bf16[16,32,128]{2,1,0:T(8,128)(2,1)S(1)}, u32[]{:S(2)}, u32[]{:S(2)}) collective-permute-start(bf16[16,32,128]{2,1,0:T(8,128)(2,1)S(1)} %slice.9.rest_0_), channel_id=1, source_target_pairs={{0,96},{2,98},{4,100},{6,102},{8,104},{10,106},{12,108},{14,110},{... | collective-permute-start | bytes 393224 | tf_op jit(solution)/shard_map/ppermute | solution.py:254
  53.0 0.4 collective-permute-start.4
  53.5 8.3 %collective-permute-done.1.rest_1_ = bf16[16,32,128]{2,1,0:T(8,128)(2,1)S(1)} collective-permute-done((bf16[16,32,128]{2,1,0:T(8,128)(2,1)S(1)}, bf16[16,32,128]{2,1,0:T(8,128)(2,1)S(1)}, u32[]{:S(2)}, u32[]{:S(2)}) %collective-permute-start.1) | collective-permute-done | bytes 131104 | tf_op jit(solution)/shard_map/ppermute | solution.py:254
  61.8 2.3 %collective-permute-start.5 = (bf16[16,32,128]{2,1,0:T(8,128)(2,1)S(1)}, bf16[16,32,128]{2,1,0:T(8,128)(2,1)S(1)}, u32[]{:S(2)}, u32[]{:S(2)}) collective-permute-start(bf16[16,32,128]{2,1,0:T(8,128)(2,1)S(1)} %slice.9.rest_0_), channel_id=1, source_target_pairs={{0,160},{2,162},{4,164},{6,166},{8,168},{10,170},{12,172},{14,174}... | collective-permute-start | bytes 393224 | tf_op jit(solution)/shard_map/ppermute | solution.py:254
  64.1 0.0 collective-permute-done.2.rest_2_
  64.1 0.7 collective-permute-start.6
  64.9 0.0 collective-permute-done.3.rest_3_
  64.9 3.7 %collective-permute-start.7 = (bf16[16,32,128]{2,1,0:T(8,128)(2,1)S(1)}, bf16[16,32,128]{2,1,0:T(8,128)(2,1)S(1)}, u32[]{:S(2)}, u32[]{:S(2)}) collective-permute-start(bf16[16,32,128]{2,1,0:T(8,128)(2,1)S(1)} %slice.9.rest_0_), channel_id=1, source_target_pairs={{0,224},{2,226},{4,228},{6,230},{8,232},{10,234},{12,236},{14,238}... | collective-permute-start | bytes 393224 | tf_op jit(solution)/shard_map/ppermute | solution.py:254
  68.5 0.0 collective-permute-done.4.rest_4_
  68.5 0.0 collective-permute-done.5.rest_5_
  68.5 0.0 copy-start.7
  68.6 1.8 %collective-permute-done.6.rest_6_ = bf16[16,32,128]{2,1,0:T(8,128)(2,1)S(1)} collective-permute-done((bf16[16,32,128]{2,1,0:T(8,128)(2,1)S(1)}, bf16[16,32,128]{2,1,0:T(8,128)(2,1)S(1)}, u32[]{:S(2)}, u32[]{:S(2)}) %collective-permute-start.6) | collective-permute-done | bytes 131104 | tf_op jit(solution)/shard_map/ppermute | solution.py:254
  70.4 4.5 %collective-permute-done.7.rest_7_ = bf16[16,32,128]{2,1,0:T(8,128)(2,1)S(1)} collective-permute-done((bf16[16,32,128]{2,1,0:T(8,128)(2,1)S(1)}, bf16[16,32,128]{2,1,0:T(8,128)(2,1)S(1)}, u32[]{:S(2)}, u32[]{:S(2)}) %collective-permute-start.7) | collective-permute-done | bytes 131104 | tf_op jit(solution)/shard_map/ppermute | solution.py:254
  74.9 0.0 collective-permute-done.win_ref
  74.9 0.0 copy-done
  75.0 0.6 copy-done.9
  75.6 0.1 copy-done.2
  75.7 21.8 %attend.1 = bf16[16,96,128]{2,1,0:T(8,128)(2,1)} custom-call(s32[1]{0:T(128)} %bitcast.place, s32[32]{0:T(128)} %lengths.1, s32[32]{0:T(128)} %groups.1, bf16[32,128]{1,0:T(8,128)(2,1)} %get-tuple-element.7.sink_ref, bf16[16,320,128]{2,1,0:T(8,128)(2,1)} %copy-done, bf16[8,192,128]{2,1,0:T(8,128)(2,1)} %copy-done.2, bf16[16,32,128]{2,1,0:T(8,128)(2,1)} %copy-done.1, ...), custom_call_target="tpu_custom_call" | custom-call | tf_op jit(solution)/shard_map/attend/pallas_call | solution.py:258
  97.5 5.7 %all-to-all-start.1 = ((bf16[16,96,128]{2,1,0:T(8,128)(2,1)}), bf16[16,96,128]{2,1,0:T(8,128)(2,1)S(1)}, u32[]{:S(2)}, u32[]{:S(2)}) async-start(bf16[16,96,128]{2,1,0:T(8,128)(2,1)} %attend.1), calls=%async_computation.1 | async-start | bytes 786432 | tf_op jit(solution)/shard_map/all_to_all | solution.py:271
  103.2 14.5 %all-to-all-done.1 = bf16[16,96,128]{2,1,0:T(8,128)(2,1)S(1)} async-done(((bf16[16,96,128]{2,1,0:T(8,128)(2,1)}), bf16[16,96,128]{2,1,0:T(8,128)(2,1)S(1)}, u32[]{:S(2)}, u32[]{:S(2)}) %all-to-all-start.1) | async-done | bytes 393248 | tf_op jit(solution)/shard_map/all_to_all | solution.py:271
  117.7 5.1 %fusion.2 = f32[128,3072]{1,0:T(8,128)S(1)} fusion(bf16[1536,128]{1,0:T(8,128)(2,1)S(1)} %bitcast.11, bf16[1536,3072]{1,0:T(8,128)(2,1)} %param.19), kind=kOutput, calls=%fused_computation.4 | convolution fusion | flops 1207959552 | bytes 11403264 | tf_op jit(solution)/shard_map/cd,cs->ds/dot_general | solution.py:273
  122.8 0.1 fusion.1
  122.9 2.8 %collective-permute-start.8 = (bf16[1536,128]{0,1:T(8,128)(2,1)S(1)}, bf16[1536,128]{0,1:T(8,128)(2,1)S(1)}, u32[]{:S(2)}, u32[]{:S(2)}) collective-permute-start(bf16[1536,128]{0,1:T(8,128)(2,1)S(1)} %fusion.1), channel_id=1, source_target_pairs={{0,1},{1,0},{2,3},{3,2},{4,5},{5,4},{6,7},{7,6},{8,9},{9,8},{10,11... | collective-permute-start | bytes 1179656 | tf_op jit(solution)/shard_map/ppermute | solution.py:277
  125.7 9.3 %collective-permute-done.8 = bf16[1536,128]{0,1:T(8,128)(2,1)S(1)} collective-permute-done((bf16[1536,128]{0,1:T(8,128)(2,1)S(1)}, bf16[1536,128]{0,1:T(8,128)(2,1)S(1)}, u32[]{:S(2)}, u32[]{:S(2)}) %collective-permute-start.8) | collective-permute-done | bytes 393248 | tf_op jit(solution)/shard_map/ppermute | solution.py:277
  135.0 0.1 fusion
  135.1 0.9 copy.11
  (17 shorter events, 0.1 us)
Async XLA Ops:
  46.0 28.9 %copy-start = (bf16[16,320,128]{2,1,0:T(8,128)(2,1)}, bf16[16,320,128]{2,1,0:T(8,128)(2,1)S(1)}, u32[]{:S(2)}) copy-start(bf16[16,320,128]{2,1,0:T(8,128)(2,1)S(1)} %all_to_all.10.own_ref) | copy-start | bytes 3932164
  46.1 28.9 %collective-permute-start = (bf16[8,192,128]{2,1,0:T(8,128)(2,1)S(1)}, bf16[8,192,128]{2,1,0:T(8,128)(2,1)S(1)}, u32[]{:S(2)}, u32[]{:S(2)}) collective-permute-start(bf16[8,192,128]{2,1,0:T(8,128)(2,1)S(1)} %slice.8), channel_id=1, source_target_pairs={{0,32},{2,34},{4,36},{6,38},{8,40},{10,42},{12,44},{14,46},{16,48}... | collective-permute-start | bytes 1179656 | tf_op jit(solution)/shard_map/ppermute | solution.py:255
  49.3 25.6 %copy-start.1 = (bf16[16,32,128]{2,1,0:T(8,128)(2,1)}, bf16[16,32,128]{2,1,0:T(8,128)(2,1)S(1)}, u32[]{:S(2)}) copy-start(bf16[16,32,128]{2,1,0:T(8,128)(2,1)S(1)} %slice.9.rest_0_) | copy-start | bytes 393220
  49.3 12.5 %collective-permute-start.1 = (bf16[16,32,128]{2,1,0:T(8,128)(2,1)S(1)}, bf16[16,32,128]{2,1,0:T(8,128)(2,1)S(1)}, u32[]{:S(2)}, u32[]{:S(2)}) collective-permute-start(bf16[16,32,128]{2,1,0:T(8,128)(2,1)S(1)} %slice.9.rest_0_), channel_id=1, source_target_pairs={{0,32},{2,34},{4,36},{6,38},{8,40},{10,42},{12,44},{14,46},{16,48}... | collective-permute-start | bytes 393224 | tf_op jit(solution)/shard_map/ppermute | solution.py:254
  50.4 13.8 %collective-permute-start.2 = (bf16[16,32,128]{2,1,0:T(8,128)(2,1)S(1)}, bf16[16,32,128]{2,1,0:T(8,128)(2,1)S(1)}, u32[]{:S(2)}, u32[]{:S(2)}) collective-permute-start(bf16[16,32,128]{2,1,0:T(8,128)(2,1)S(1)} %slice.9.rest_0_), channel_id=1, source_target_pairs={{0,64},{2,66},{4,68},{6,70},{8,72},{10,74},{12,76},{14,78},{16,80}... | collective-permute-start | bytes 393224 | tf_op jit(solution)/shard_map/ppermute | solution.py:254
  51.3 13.5 %collective-permute-start.3 = (bf16[16,32,128]{2,1,0:T(8,128)(2,1)S(1)}, bf16[16,32,128]{2,1,0:T(8,128)(2,1)S(1)}, u32[]{:S(2)}, u32[]{:S(2)}) collective-permute-start(bf16[16,32,128]{2,1,0:T(8,128)(2,1)S(1)} %slice.9.rest_0_), channel_id=1, source_target_pairs={{0,96},{2,98},{4,100},{6,102},{8,104},{10,106},{12,108},{14,110},{... | collective-permute-start | bytes 393224 | tf_op jit(solution)/shard_map/ppermute | solution.py:254
  53.0 15.5 %collective-permute-start.4 = (bf16[16,32,128]{2,1,0:T(8,128)(2,1)S(1)}, bf16[16,32,128]{2,1,0:T(8,128)(2,1)S(1)}, u32[]{:S(2)}, u32[]{:S(2)}) collective-permute-start(bf16[16,32,128]{2,1,0:T(8,128)(2,1)S(1)} %slice.9.rest_0_), channel_id=1, source_target_pairs={{0,128},{2,130},{4,132},{6,134},{8,136},{10,138},{12,140},{14,142}... | collective-permute-start | bytes 393224 | tf_op jit(solution)/shard_map/ppermute | solution.py:254
  61.8 13.1 %copy-start.3 = (bf16[16,32,128]{2,1,0:T(8,128)(2,1)}, bf16[16,32,128]{2,1,0:T(8,128)(2,1)S(1)}, u32[]{:S(2)}) copy-start(bf16[16,32,128]{2,1,0:T(8,128)(2,1)S(1)} %collective-permute-done.1.rest_1_) | copy-start | bytes 393220
  61.8 6.7 %collective-permute-start.5 = (bf16[16,32,128]{2,1,0:T(8,128)(2,1)S(1)}, bf16[16,32,128]{2,1,0:T(8,128)(2,1)S(1)}, u32[]{:S(2)}, u32[]{:S(2)}) collective-permute-start(bf16[16,32,128]{2,1,0:T(8,128)(2,1)S(1)} %slice.9.rest_0_), channel_id=1, source_target_pairs={{0,160},{2,162},{4,164},{6,166},{8,168},{10,170},{12,172},{14,174}... | collective-permute-start | bytes 393224 | tf_op jit(solution)/shard_map/ppermute | solution.py:254
  64.1 10.8 %copy-start.4 = (bf16[16,32,128]{2,1,0:T(8,128)(2,1)}, bf16[16,32,128]{2,1,0:T(8,128)(2,1)S(1)}, u32[]{:S(2)}) copy-start(bf16[16,32,128]{2,1,0:T(8,128)(2,1)S(1)} %collective-permute-done.2.rest_2_) | copy-start | bytes 393220
  64.1 6.2 %collective-permute-start.6 = (bf16[16,32,128]{2,1,0:T(8,128)(2,1)S(1)}, bf16[16,32,128]{2,1,0:T(8,128)(2,1)S(1)}, u32[]{:S(2)}, u32[]{:S(2)}) collective-permute-start(bf16[16,32,128]{2,1,0:T(8,128)(2,1)S(1)} %slice.9.rest_0_), channel_id=1, source_target_pairs={{0,192},{2,194},{4,196},{6,198},{8,200},{10,202},{12,204},{14,206}... | collective-permute-start | bytes 393224 | tf_op jit(solution)/shard_map/ppermute | solution.py:254
  64.9 10.1 %copy-start.5 = (bf16[16,32,128]{2,1,0:T(8,128)(2,1)}, bf16[16,32,128]{2,1,0:T(8,128)(2,1)S(1)}, u32[]{:S(2)}) copy-start(bf16[16,32,128]{2,1,0:T(8,128)(2,1)S(1)} %collective-permute-done.3.rest_3_) | copy-start | bytes 393220
  64.9 10.0 %collective-permute-start.7 = (bf16[16,32,128]{2,1,0:T(8,128)(2,1)S(1)}, bf16[16,32,128]{2,1,0:T(8,128)(2,1)S(1)}, u32[]{:S(2)}, u32[]{:S(2)}) collective-permute-start(bf16[16,32,128]{2,1,0:T(8,128)(2,1)S(1)} %slice.9.rest_0_), channel_id=1, source_target_pairs={{0,224},{2,226},{4,228},{6,230},{8,232},{10,234},{12,236},{14,238}... | collective-permute-start | bytes 393224 | tf_op jit(solution)/shard_map/ppermute | solution.py:254
  68.5 6.4 %copy-start.6 = (bf16[16,32,128]{2,1,0:T(8,128)(2,1)}, bf16[16,32,128]{2,1,0:T(8,128)(2,1)S(1)}, u32[]{:S(2)}) copy-start(bf16[16,32,128]{2,1,0:T(8,128)(2,1)S(1)} %collective-permute-done.4.rest_4_) | copy-start | bytes 393220
  68.5 6.4 %copy-start.7 = (bf16[16,32,128]{2,1,0:T(8,128)(2,1)}, bf16[16,32,128]{2,1,0:T(8,128)(2,1)S(1)}, u32[]{:S(2)}) copy-start(bf16[16,32,128]{2,1,0:T(8,128)(2,1)S(1)} %collective-permute-done.5.rest_5_) | copy-start | bytes 393220
  70.3 4.6 %copy-start.8 = (bf16[16,32,128]{2,1,0:T(8,128)(2,1)}, bf16[16,32,128]{2,1,0:T(8,128)(2,1)S(1)}, u32[]{:S(2)}) copy-start(bf16[16,32,128]{2,1,0:T(8,128)(2,1)S(1)} %collective-permute-done.6.rest_6_) | copy-start | bytes 393220
  74.9 0.7 copy-start.9
  74.9 0.8 copy-start.2
  97.5 20.2 %all-to-all-start.1 = ((bf16[16,96,128]{2,1,0:T(8,128)(2,1)}), bf16[16,96,128]{2,1,0:T(8,128)(2,1)S(1)}, u32[]{:S(2)}, u32[]{:S(2)}) async-start(bf16[16,96,128]{2,1,0:T(8,128)(2,1)} %attend.1), calls=%async_computation.1 | async-start | bytes 786432 | tf_op jit(solution)/shard_map/all_to_all | solution.py:271
  122.9 12.1 %collective-permute-start.8 = (bf16[1536,128]{0,1:T(8,128)(2,1)S(1)}, bf16[1536,128]{0,1:T(8,128)(2,1)S(1)}, u32[]{:S(2)}, u32[]{:S(2)}) collective-permute-start(bf16[1536,128]{0,1:T(8,128)(2,1)S(1)} %fusion.1), channel_id=1, source_target_pairs={{0,1},{1,0},{2,3},{3,2},{4,5},{5,4},{6,7},{7,6},{8,9},{9,8},{10,11... | collective-permute-start | bytes 1179656 | tf_op jit(solution)/shard_map/ppermute | solution.py:277

commit v2 on v1

v2 whole, which is shorter than its diff:
```python
import functools
import math

import jax
import jax.numpy as jnp
from jax import lax
from jax.experimental import pallas as pl
from jax.experimental.pallas import tpu as pltpu
from jax.sharding import PartitionSpec as P

HD = 96
W = 1024
SINKS = 4
G = 2
RING = 16
BLK = 128
QB = 256
CH = 256
LANES = 128
FAR = 1 << 28
LOW = -1e30
VMEM_LIMIT = 24 << 20


def pack_kernel(head, q_ref, k_ref, v_ref, ck_ref, cv_ref, sk_ref, sv_ref, query_ref, out_ref, sink_ref):
    heads = q_ref.shape[1] // HD
    for which, ref in enumerate((k_ref, v_ref, q_ref)):
        turned = ref[...].T
        for p in range(heads):
            piece = turned[p * HD : (p + 1) * HD, :]
            if which == 2:
                query_ref[p] = piece
            else:
                out_ref[p, which * HD : (which + 1) * HD, :] = piece
    rows = ck_ref.shape[0]
    fill = jnp.zeros((rows, LANES - HD), ck_ref.dtype)
    for which, ref in enumerate((ck_ref, cv_ref)):
        for p in range(heads):
            piece = jnp.concatenate([ref[:, p * HD : (p + 1) * HD], fill], axis=1)
            base = 2 * HD + which * rows
            out_ref[p, base : base + rows, :] = piece
    width = sk_ref.shape[1]
    column = lax.broadcasted_iota(jnp.int32, (width, LANES), 0)
    lane = lax.broadcasted_iota(jnp.int32, (width, LANES), 1)
    pick = ((column == head[0] * HD + lane) & (lane < HD)).astype(jnp.float32).astype(jnp.bfloat16)
    for which, ref in enumerate((sk_ref, sv_ref)):
        piece = jnp.dot(ref[...], pick, preferred_element_type=jnp.float32)
        piece = jnp.concatenate([piece, jnp.zeros_like(piece)], axis=0)
        sink_ref[which * 16 : (which + 1) * 16, :] = piece.astype(jnp.bfloat16)


def gather_facts(place, lengths, groups, need, blocks):
    base = place[0] * RING * BLK
    own = RING * BLK
    for b in range((1 + G) * blocks):
        need[b] = FAR

    def one_request(r, carry):
        start, start_col, group_col = carry
        length = lengths[r]
        group = groups[r]
        first = jnp.where(start < base, 0, (start - base) // QB)
        last = jnp.minimum((start + length - 1 - base) // QB, blocks - 1)

        def mark(b, _):
            need[b] = jnp.minimum(need[b], start)
            offset = jnp.maximum(base + b * QB - start, 0)
            at = (1 + group) * blocks + b
            need[at] = jnp.minimum(need[at], offset)
            return 0

        @pl.when((start < base + own) & (start + length > base))
        def _():
            lax.fori_loop(first, last + 1, mark, 0)

        row = lax.broadcasted_iota(jnp.int32, start_col.shape, 0)
        start_col = jnp.where(row == r, start, start_col)
        group_col = jnp.where(row == r, group, group_col)
        return (start + length, start_col, group_col)

    reqs = lengths.shape[0]
    column = jnp.zeros((reqs, QB), jnp.int32)
    _, start_col, group_col = lax.fori_loop(0, reqs, one_request, (jnp.int32(0), column, column))
    return base, start_col, group_col


def query_facts(index, start_col, group_col):
    begun = start_col <= index
    start_q = jnp.max(jnp.where(begun, start_col, 0), axis=0, keepdims=True)
    here = begun & (start_col == start_q)
    group_q = jnp.max(jnp.where(here, group_col, 0), axis=0, keepdims=True)
    return jnp.maximum(start_q, index - (W - 1)), index - start_q, group_q


def turn(piece):
    pad = jnp.zeros((LANES - HD, BLK), jnp.bfloat16)
    return jnp.concatenate([piece, pad], axis=0).T


def query_block(query_ref, b):
    q_t = jnp.concatenate([query_ref[2 * b], query_ref[2 * b + 1]], axis=1)
    return jnp.concatenate([q_t, jnp.zeros((LANES - HD, QB), jnp.bfloat16)], axis=0)


def values(val_ref, at):
    slot = at // BLK
    return jnp.concatenate([val_ref[slot], val_ref[slot + 1]], axis=1)


def dot(a, b):
    return jnp.dot(a, b, preferred_element_type=jnp.float32)


FACTOR = (1.0 / math.sqrt(HD)) * math.log2(math.e)


def prep_kernel(place, lengths, groups, own_ref, key_ref, low_ref, need):
    for j in range(RING):
        key_ref[j * BLK : (j + 1) * BLK, :] = turn(own_ref[j, 0:HD, :])
    own = RING * BLK
    blocks = own // QB
    cache_at = W + own
    base, start_col, group_col = gather_facts(place, lengths, groups, need, blocks)
    lane = lax.broadcasted_iota(jnp.int32, (1, QB), 1)
    for b in range(blocks):
        index = base + b * QB + lane
        low_q, offset, group_q = query_facts(index, start_col, group_col)
        low_ref[b, 0:1, :] = low_q - base + W
        for g in range(G):
            low_ref[b, 1 + g : 2 + g, :] = jnp.where(
                group_q == g, cache_at + g * W + offset + 1, FAR
            )
        low_ref[b, 1 + G : 2 + G, :] = jnp.full((1, QB), FAR, jnp.int32)
        low_ref[b, 2 + G : 3 + G, :] = group_q


def attend_kernel(
    place, need, low_ref, sink_ref, query_ref, own_ref, turned_ref, win_ref, *rest, rings
):
    caches = rest[:rings]
    out_ref, key_ref, val_ref = rest[rings:]
    ring = place[0]
    base = ring * RING * BLK
    front = W
    own = RING * BLK
    cache_at = front + own
    blocks = own // QB
    for j in range(RING // 2):
        key_ref[j * BLK : (j + 1) * BLK, :] = turn(win_ref[j, 0:HD, :])
        val_ref[j] = win_ref[j, HD : 2 * HD, :]
    key_ref[front : front + own, :] = turned_ref[...]
    for j in range(RING):
        val_ref[front // BLK + j] = own_ref[j, HD : 2 * HD, :]
    rows = RING * 16
    for k in range(rings):
        source = lax.rem(lax.rem(ring, 4) + k % 4, 4) + 4 * lax.rem(ring // 4 + k // 4, 2)
        piece = caches[k][...]
        at = pl.multiple_of(cache_at + source * rows, rows)
        key_ref[pl.ds(at, rows), :] = piece[:, 0:16, :].reshape(rows, LANES)
        turned = piece[:, 16:32, :].reshape(rows, LANES).T
        for half in range(rows // BLK):
            val_ref[at // BLK + half] = turned[0:HD, half * BLK : (half + 1) * BLK]
    lane = lax.broadcasted_iota(jnp.int32, (1, QB), 1)
    row_iota = lax.broadcasted_iota(jnp.int32, (CH, QB), 0)
    sink_row = lax.broadcasted_iota(jnp.int32, (16, QB), 0)
    sink_v = sink_ref[16:32, :].T[0:HD, :]

    def one_block(b, _):
        low_suffix = low_ref[b, 0:1, :]
        group_q = low_ref[b, 2 + G : 3 + G, :]
        q_t = query_block(query_ref, b)
        at0 = pl.multiple_of(front + b * QB, CH)
        s_d = dot(key_ref[pl.ds(at0, CH), :], q_t)
        s_d = jnp.where((row_iota >= low_suffix - at0) & (row_iota <= lane), s_d, LOW)
        s_s = dot(sink_ref[0:16, :], q_t)
        s_s = jnp.where((sink_row // SINKS == group_q) & (sink_row < G * SINKS), s_s, LOW)
        top = jnp.maximum(jnp.max(s_d, axis=0, keepdims=True), jnp.max(s_s, axis=0, keepdims=True))
        p_d = jnp.exp2((s_d - top) * FACTOR)
        p_s = jnp.exp2((s_s - top) * FACTOR)
        den = jnp.sum(p_d, axis=0, keepdims=True) + jnp.sum(p_s, axis=0, keepdims=True)
        acc = dot(values(val_ref, at0), p_d.astype(jnp.bfloat16))
        acc = acc + dot(sink_v, p_s.astype(jnp.bfloat16))

        first = (jnp.maximum(need[b] - base, b * QB - (W - 1)) + front) // CH
        n_suffix = front // CH + b - first
        c0 = [jnp.minimum((need[(1 + g) * blocks + b] + 1) // CH, W // CH) for g in range(G)]
        n0, n1 = [W // CH - c for c in c0]
        total = n_suffix + n0 + n1

        def where_is(j):
            in0 = j - n_suffix
            in1 = in0 - n0
            at = jnp.where(
                in0 < 0,
                (first + j) * CH,
                jnp.where(
                    in1 < 0,
                    cache_at + (c0[0] + in0) * CH,
                    jnp.where(j < total, cache_at + W + (c0[1] + in1) * CH, 0),
                ),
            )
            kind = jnp.where(in0 < 0, 0, jnp.where(in1 < 0, 1, jnp.where(j < total, 2, 3)))
            return pl.multiple_of(at, CH), kind

        def step(j, state):
            top, den, acc = state
            scores, ats = [], []
            for u in range(2):
                at, kind = where_is(2 * j + u)
                s = dot(key_ref[pl.ds(at, CH), :], q_t)
                low = low_ref[b, pl.ds(kind, 1), :] - at
                scores.append(jnp.where(row_iota >= low, s, LOW))
                ats.append(at)
            new = jnp.maximum(
                jnp.max(scores[0], axis=0, keepdims=True),
                jnp.max(scores[1], axis=0, keepdims=True),
            )
            new = jnp.maximum(top, new)
            fade = jnp.exp2((top - new) * FACTOR)
            den = den * fade
            ps = []
            for u in range(2):
                p = jnp.exp2((scores[u] - new) * FACTOR)
                den = den + jnp.sum(p, axis=0, keepdims=True)
                ps.append(p.astype(jnp.bfloat16))
            vals = jnp.concatenate([values(val_ref, at) for at in ats], axis=1)
            acc = acc * fade + dot(vals, jnp.concatenate(ps, axis=0))
            return (new, den, acc)

        _, den, acc = lax.fori_loop(0, (total + 1) // 2, step, (top, den, acc))
        done = (acc / den).astype(jnp.bfloat16)
        out_ref[2 * b] = done[:, 0:BLK]
        out_ref[2 * b + 1] = done[:, BLK:QB]
        return 0

    lax.fori_loop(0, blocks, one_block, 0)


def project_here_kernel(side, attn_ref, w_ref, out_ref, half_ref, arrived):
    features = half_ref.shape[1]
    columns = pl.ds(pl.multiple_of(side[0] * features, features), features)
    parts = arrived.shape[0]
    tall = half_ref.shape[0] // parts
    loads = [
        pltpu.make_async_copy(
            w_ref.at[pl.ds(n * tall, tall), columns],
            half_ref.at[pl.ds(n * tall, tall), :],
            arrived.at[n],
        )
        for n in range(parts)
    ]
    for load in loads:
        load.start()
    turned = attn_ref[...].T
    for load in loads:
        load.wait()
    piece = 256
    for j in range(features // piece):
        at = slice(j * piece, (j + 1) * piece)
        out_ref[at, :] = dot(turned, half_ref[:, at]).T.astype(out_ref.dtype)


def project_kernel(side, attn_ref, w_ref, out_ref, turned_ref):
    @pl.when(pl.program_id(0) == 0)
    def _():
        turned_ref[...] = attn_ref[...].T

    out_ref[...] = dot(turned_ref[...], w_ref[...]).T.astype(out_ref.dtype)


def project_cost(width, features, rows):
    return pl.CostEstimate(
        flops=2 * width * features * rows, bytes_accessed=2 * width * features, transcendentals=0
    )


def project_here(side, attn_t, w_out):
    width, rows = attn_t.shape
    features = w_out.shape[1] // 2
    return pl.pallas_call(
        project_here_kernel,
        out_shape=jax.ShapeDtypeStruct((features, rows), jnp.bfloat16),
        in_specs=[smem(), vmem(), pl.BlockSpec(memory_space=pltpu.HBM)],
        out_specs=vmem(),
        scratch_shapes=[
            pltpu.VMEM((width, features), jnp.bfloat16),
            pltpu.SemaphoreType.DMA((12,)),
        ],
        cost_estimate=project_cost(width, features, rows),
        compiler_params=pltpu.CompilerParams(vmem_limit_bytes=VMEM_LIMIT),
        name="project_here",
    )(side.reshape(1), attn_t, w_out)


def project(side, attn_t, w_out):
    width, rows = attn_t.shape
    features = w_out.shape[1] // 2
    piece = 512
    steps = features // piece
    return pl.pallas_call(
        project_kernel,
        out_shape=jax.ShapeDtypeStruct((features, rows), jnp.float32),
        grid_spec=pltpu.PrefetchScalarGridSpec(
            num_scalar_prefetch=1,
            grid=(steps,),
            in_specs=[
                pl.BlockSpec((width, rows), lambda j, side: (0, 0)),
                pl.BlockSpec((width, piece), lambda j, side: (0, side[0] * steps + j)),
            ],
            out_specs=pl.BlockSpec((piece, rows), lambda j, side: (j, 0)),
            scratch_shapes=[pltpu.VMEM((rows, width), jnp.bfloat16)],
        ),
        cost_estimate=project_cost(width, features, rows),
        name="project",
    )(side.reshape(1), attn_t, w_out)


def vmem():
    return pl.BlockSpec(memory_space=pltpu.VMEM)


def smem():
    return pl.BlockSpec(memory_space=pltpu.SMEM)


def shards(
    queries, keys, values, cache_k, cache_v, sink_k, sink_v, suffix_lengths, request_group, w_out
):
    rows, width = queries.shape
    heads = width // HD
    seq = lax.axis_size("seq")
    rings = seq // RING
    device = lax.axis_index("seq")
    half = lax.axis_index("head")
    packed_q, packed, sinks = pl.pallas_call(
        pack_kernel,
        out_shape=(
            jax.ShapeDtypeStruct((heads, HD, LANES), jnp.bfloat16),
            jax.ShapeDtypeStruct((heads, 2 * HD + 32, LANES), jnp.bfloat16),
            jax.ShapeDtypeStruct((32, LANES), jnp.bfloat16),
        ),
        in_specs=[smem()] + [vmem()] * 7,
        out_specs=(vmem(), vmem(), vmem()),
        name="pack",
    )(
        (device % RING).reshape(1), queries, keys, values, cache_k, cache_v, sink_k, sink_v
    )
    members = [[r * RING + i for i in range(RING)] for r in range(rings)]

    def trade(array, groups):
        return lax.all_to_all(array, "seq", 0, 0, axis_index_groups=groups, tiled=True)

    mine = trade(packed, members)
    mine_q = trade(packed_q, members)
    window = lax.ppermute(
        mine[RING // 2 :, : 2 * HD, :], "seq", [(s, s + RING) for s in range(seq - RING)]
    )
    cache = mine[:, 2 * HD :, :]

    def send(array, dx, dy):
        pairs = []
        for r in range(rings):
            to = (r % 4 + dy) % 4 + 4 * ((r // 4 + dx) % 2)
            pairs += [(r * RING + i, to * RING + i) for i in range(RING)]
        return lax.ppermute(array, "seq", pairs)

    near_y = send(cache, 0, 3)
    near_x = send(cache, 1, 0)
    back_y = send(cache, 0, 1)
    far_y = send(near_y, 0, 3)
    near_xy = send(near_x, 0, 3)
    back_xy = send(back_y, 1, 0)
    far_xy = send(far_y, 1, 0)
    caches = [cache, near_y, far_y, back_y, near_x, near_xy, far_xy, back_xy]
    own = RING * BLK
    blocks = own // QB
    total = W + own + G * W
    place = (device // RING).reshape(1)
    turned, lows, need = pl.pallas_call(
        prep_kernel,
        out_shape=(
            jax.ShapeDtypeStruct((own, LANES), jnp.bfloat16),
            jax.ShapeDtypeStruct((blocks, 8, QB), jnp.int32),
            jax.ShapeDtypeStruct(((1 + G) * blocks,), jnp.int32),
        ),
        in_specs=[smem()] * 3 + [vmem()],
        out_specs=(vmem(), vmem(), smem()),
        cost_estimate=pl.CostEstimate(
            flops=1 << 20, bytes_accessed=1 << 22, transcendentals=0
        ),
        compiler_params=pltpu.CompilerParams(vmem_limit_bytes=VMEM_LIMIT),
        name="prep",
    )(place, suffix_lengths, request_group, mine)
    attn = pl.pallas_call(
        functools.partial(attend_kernel, rings=rings),
        out_shape=jax.ShapeDtypeStruct((RING, HD, BLK), jnp.bfloat16),
        in_specs=[smem()] * 2 + [vmem()] * (6 + rings),
        out_specs=vmem(),
        scratch_shapes=[
            pltpu.VMEM((total, LANES), jnp.bfloat16),
            pltpu.VMEM((total // BLK, HD, BLK), jnp.bfloat16),
        ],
        compiler_params=pltpu.CompilerParams(vmem_limit_bytes=VMEM_LIMIT),
        name="attend",
    )(place, need, lows, sinks, mine_q, mine, turned, window, *caches)
    attn_t = trade(attn, members).reshape(width, rows)
    give = project_here(1 - half, attn_t, w_out)
    got = lax.ppermute(give, "head", [(0, 1), (1, 0)])
    keep = project(half, attn_t, w_out)
    return (keep + got.astype(jnp.float32)).astype(jnp.bfloat16)


def solution(mesh):
    placed = (
        P("seq", "head"),
        P("seq", "head"),
        P("seq", "head"),
        P("seq", "head"),
        P("seq", "head"),
        P(None, "head"),
        P(None, "head"),
        P(),
        P(),
        P("head", None),
    )
    return jax.shard_map(
        shards, mesh=mesh, in_specs=placed, out_specs=P("head", "seq"), check_vma=False
    )
```

time: 136 us -> 132 us (0.971)
  the two profiles are of different devices: /device:TPU:9 before, /device:TPU:3 now
where the time goes in v2:
time: 132 us; the launch traced here: 131 us
  blocking collectives  34.8 us (26%)
  starting transfers between devices  34.5 us (26%)
  Pallas kernels  30.4 us (23%)
  waiting for transfers between devices  23 us (17%)
  local copies, waits for them, and re-layouts  6.61 us (5%)
  other arithmetic  1.96 us (1%)
    all_to_all x1, blocking collectives, trade(): lax.all_to_all(array, 'seq', 0, 0, axis_index_groups=groups, tiled=True)  34.8 us
    ppermute x7, starting transfers between devices, send(): return lax.ppermute(array, 'seq', pairs)  19 us
    pallas_call x1, Pallas kernels, shards(): pl.pallas_call(functools.partial(attend_kernel, rings=rings), out_shape=j...  18.9 us
    all_to_all x2, waiting for transfers between devices, trade(): lax.all_to_all(array, 'seq', 0, 0, axis_index_groups=groups, tiled=True)  14.5 us
    all_to_all x2, starting transfers between devices, trade(): lax.all_to_all(array, 'seq', 0, 0, axis_index_groups=groups, tiled=True)  11.6 us
    unnamed x10, local copies, waits for them, and re-layouts  5.83 us
    ppermute x1, waiting for transfers between devices, shards(): got = lax.ppermute(give, 'head', [(0, 1), (1, 0)])  5.31 us
    pallas_call x1, Pallas kernels, project(): pl.pallas_call(project_kernel, out_shape=jax.ShapeDtypeStruct((features,...  4.9 us
  transfers between devices with their start and end apart: 11, of which 5 were waited for; matrix products, arithmetic and copies ran while one was open for 1% of the time, Pallas kernels for 5%

profile of v2, /device:TPU:3, one launch (start us, length us, event | category | flops | bytes accessed | tf_op | source)
XLA Modules:
  0.0 131.3 jit_solution(98160799029302771)
XLA Ops:
  0.0 2.7 %pack.1 = (bf16[16,96,128]{2,1,0:T(8,128)(2,1)}, bf16[16,224,128]{2,1,0:T(8,128)(2,1)}, bf16[32,128]{1,0:T(8,128)(2,1)}) custom-call(s32[1]{0:T(128)} %bitcast.2.head, bf16[128,1536]{1,0:T(8,128)(2,1)} %q_ref.1, bf16[128,1536]{1,0:T(8,128)(2,1)} %k_ref.1, bf16[128,1536]{1,0:T(8,128)(2,1)} %v_ref.1, bf16[16,1536]{1,0:T(8,128)(2,1)} %ck_ref.1, ...), custom_call_target="tpu_custom_call" | custom-call | tf_op jit(solution)/shard_map/pack/pallas_call | solution.py:335
  2.7 34.8 %all_to_all.15.own_ref = bf16[16,224,128]{2,1,0:T(8,128)(2,1)S(1)} all-to-all(bf16[16,224,128]{2,1,0:T(8,128)(2,1)} %get-tuple-element.11), channel_id=1, replica_groups={{0,2,4,6,8,10,12,14,16,18,20,22,24,26,28,30},{32,34,36,38,40,42,44,46,4..., dimensions={0} | all-to-all | bytes 1835008 | tf_op jit(solution)/shard_map/all_to_all | solution.py:351
  37.5 3.5 %all-to-all-start.1 = ((bf16[16,96,128]{2,1,0:T(8,128)(2,1)}), bf16[16,96,128]{2,1,0:T(8,128)(2,1)S(1)}, u32[]{:S(2)}, u32[]{:S(2)}) async-start(bf16[16,96,128]{2,1,0:T(8,128)(2,1)} %get-tuple-element.15), calls=%async_computation.1 | async-start | bytes 786432 | tf_op jit(solution)/shard_map/all_to_all | solution.py:351
  41.0 2.8 %collective-permute-start.1 = (bf16[16,32,128]{2,1,0:T(8,128)(2,1)S(1)}, bf16[16,32,128]{2,1,0:T(8,128)(2,1)S(1)}, u32[]{:S(2)}, u32[]{:S(2)}) collective-permute-start(bf16[16,32,128]{2,1,0:T(8,128)(2,1)S(1)} %slice.9.rest_0_), channel_id=1, source_target_pairs={{0,96},{2,98},{4,100},{6,102},{8,104},{10,106},{12,108},{14,110},{... | collective-permute-start | bytes 393224 | tf_op jit(solution)/shard_map/ppermute | solution.py:365
  43.8 0.8 slice.8
  44.6 1.9 %collective-permute-start = (bf16[8,192,128]{2,1,0:T(8,128)(2,1)}, bf16[8,192,128]{2,1,0:T(8,128)(2,1)S(1)}, u32[]{:S(2)}, u32[]{:S(2)}) collective-permute-start(bf16[8,192,128]{2,1,0:T(8,128)(2,1)} %slice.8), channel_id=1, source_target_pairs={{0,32},{2,34},{4,36},{6,38},{8,40},{10,42},{12,44},{14,46},{16,48}... | collective-permute-start | bytes 1179656 | tf_op jit(solution)/shard_map/ppermute | solution.py:355
  46.5 0.1 collective-permute-start.4
  46.6 0.3 collective-permute-start.3
  46.8 0.2 collective-permute-done.1.rest_1_
  47.0 3.4 %collective-permute-start.2 = (bf16[16,32,128]{2,1,0:T(8,128)(2,1)S(1)}, bf16[16,32,128]{2,1,0:T(8,128)(2,1)S(1)}, u32[]{:S(2)}, u32[]{:S(2)}) collective-permute-start(bf16[16,32,128]{2,1,0:T(8,128)(2,1)S(1)} %collective-permute-done.1.rest_1_), channel_id=1, source_target_pairs={{0,96},{2,98},{4,100},{6,102},{8,104},{10,106},{12,108},{14,110},{... | collective-permute-start | bytes 393224 | tf_op jit(solution)/shard_map/ppermute | solution.py:365
  50.4 1.3 collective-permute-done.4.rest_4_
  51.7 11.0 %collective-permute-start.5 = (bf16[16,32,128]{2,1,0:T(8,128)(2,1)S(1)}, bf16[16,32,128]{2,1,0:T(8,128)(2,1)S(1)}, u32[]{:S(2)}, u32[]{:S(2)}) collective-permute-start(bf16[16,32,128]{2,1,0:T(8,128)(2,1)S(1)} %collective-permute-done.4.rest_4_), channel_id=1, source_target_pairs={{0,96},{2,98},{4,100},{6,102},{8,104},{10,106},{12,108},{14,110},{... | collective-permute-start | bytes 393224 | tf_op jit(solution)/shard_map/ppermute | solution.py:365
  62.7 0.0 collective-permute-done.3.rest_3_
  62.7 0.0 collective-permute-start.7
  62.7 1.5 %collective-permute-start.6 = (bf16[16,32,128]{2,1,0:T(8,128)(2,1)S(1)}, bf16[16,32,128]{2,1,0:T(8,128)(2,1)S(1)}, u32[]{:S(2)}, u32[]{:S(2)}) collective-permute-start(bf16[16,32,128]{2,1,0:T(8,128)(2,1)S(1)} %collective-permute-done.2.rest_2_), channel_id=1, source_target_pairs={{0,128},{2,130},{4,132},{6,134},{8,136},{10,138},{12,140},{14,142}... | collective-permute-start | bytes 393224 | tf_op jit(solution)/shard_map/ppermute | solution.py:365
  64.2 0.7 copy-done.3
  64.8 0.7 copy-done.4
  65.5 2.3 %prep.1 = (bf16[2048,128]{1,0:T(8,128)(2,1)S(1)}, s32[8,8,256]{2,1,0:T(8,128)S(1)}, s32[24]{0:T(128)S(1)}) custom-call(s32[1]{0:T(128)} %bitcast.1.place, s32[32]{0:T(128)S(1)} %copy-done.3, s32[32]{0:T(128)S(1)} %copy-done.4, bf16[16,224,128]{2,1,0:T(8,128)(2,1)S(1)} %all_to_all.15.own_ref), custom_call_target="tpu_custom_call" | custom-call | flops 1048576 | bytes 4194304 | tf_op jit(solution)/shard_map/prep/pallas_call | solution.py:379
  67.7 0.0 all-to-all-done.1.query_ref
  67.7 0.0 collective-permute-done.7.rest_7_
  67.8 0.0 collective-permute-done.win_ref
  67.8 1.7 %collective-permute-done.6.rest_6_ = bf16[16,32,128]{2,1,0:T(8,128)(2,1)S(1)} collective-permute-done((bf16[16,32,128]{2,1,0:T(8,128)(2,1)S(1)}, bf16[16,32,128]{2,1,0:T(8,128)(2,1)S(1)}, u32[]{:S(2)}, u32[]{:S(2)}) %collective-permute-start.6) | collective-permute-done | bytes 131104 | tf_op jit(solution)/shard_map/ppermute | solution.py:365
  69.5 0.7 copy-done.2
  70.2 18.9 %attend.1 = bf16[16,96,128]{2,1,0:T(8,128)(2,1)} custom-call(s32[1]{0:T(128)} %bitcast.1.place, s32[24]{0:T(128)S(1)} %get-tuple-element.12.need, s32[8,8,256]{2,1,0:T(8,128)S(1)} %get-tuple-element.13.low_ref, bf16[32,128]{1,0:T(8,128)(2,1)S(1)} %copy-done.2, bf16[16,96,128]{2,1,0:T(8,128)(2,1)S(1)} %all-to-all-done.1.query_ref, ...), custom_call_target="tpu_custom_call" | custom-call | tf_op jit(solution)/shard_map/attend/pallas_call | solution.py:394
  89.1 8.2 %all-to-all-start.2 = ((bf16[16,96,128]{2,1,0:T(8,128)(2,1)}), bf16[16,96,128]{2,1,0:T(8,128)(2,1)S(1)}, u32[]{:S(2)}, u32[]{:S(2)}) async-start(bf16[16,96,128]{2,1,0:T(8,128)(2,1)} %attend.1), calls=%async_computation.2 | async-start | bytes 786432 | tf_op jit(solution)/shard_map/all_to_all | solution.py:351
  97.3 14.5 %all-to-all-done.2 = bf16[16,96,128]{2,1,0:T(8,128)(2,1)S(1)} async-done(((bf16[16,96,128]{2,1,0:T(8,128)(2,1)}), bf16[16,96,128]{2,1,0:T(8,128)(2,1)S(1)}, u32[]{:S(2)}, u32[]{:S(2)}) %all-to-all-start.2) | async-done | bytes 393248 | tf_op jit(solution)/shard_map/all_to_all | solution.py:351
  111.8 3.8 %copy-done = bf16[1536,3072]{1,0:T(8,128)(2,1)S(1)} copy-done((bf16[1536,3072]{1,0:T(8,128)(2,1)S(1)}, bf16[1536,3072]{1,0:T(8,128)(2,1)}, u32[]{:S(2)}) %copy-start) | copy-done | bytes 9437208
  115.6 1.6 %project_here.1 = bf16[1536,128]{1,0:T(8,128)(2,1)S(1)} custom-call(s32[1]{0:T(128)} %bitcast.4.side, bf16[1536,128]{1,0:T(8,128)(2,1)S(1)} %bitcast.5, bf16[1536,3072]{1,0:T(8,128)(2,1)S(1)} %copy-done), custom_call_target="tpu_custom_call" | custom-call | flops 603979776 | bytes 4718592 | tf_op jit(solution)/shard_map/project_here/pallas_call | solution.py:280
  117.2 1.9 %collective-permute-start.8 = (bf16[1536,128]{1,0:T(8,128)(2,1)S(1)}, bf16[1536,128]{1,0:T(8,128)(2,1)S(1)}, u32[]{:S(2)}, u32[]{:S(2)}) collective-permute-start(bf16[1536,128]{1,0:T(8,128)(2,1)S(1)} %project_here.1), channel_id=1, source_target_pairs={{0,1},{1,0},{2,3},{3,2},{4,5},{5,4},{6,7},{7,6},{8,9},{9,8},{10,11... | collective-permute-start | bytes 1179656 | tf_op jit(solution)/shard_map/ppermute | solution.py:408
  119.1 4.9 %project.1 = f32[1536,128]{1,0:T(8,128)} custom-call(s32[1]{0:T(128)} %bitcast.side, bf16[1536,128]{1,0:T(8,128)(2,1)} %bitcast.6, bf16[1536,3072]{1,0:T(8,128)(2,1)} %w_ref.3), custom_call_target="tpu_custom_call" | custom-call | flops 603979776 | bytes 4718592 | tf_op jit(solution)/shard_map/project/pallas_call | solution.py:300
  124.0 5.3 %collective-permute-done.8 = bf16[1536,128]{1,0:T(8,128)(2,1)S(1)} collective-permute-done((bf16[1536,128]{1,0:T(8,128)(2,1)S(1)}, bf16[1536,128]{1,0:T(8,128)(2,1)S(1)}, u32[]{:S(2)}, u32[]{:S(2)}) %collective-permute-start.8) | collective-permute-done | bytes 393248 | tf_op jit(solution)/shard_map/ppermute | solution.py:408
  129.4 2.0 %add_convert_fusion = bf16[1536,128]{1,0:T(8,128)(2,1)} fusion(f32[1536,128]{1,0:T(8,128)} %project.1, bf16[1536,128]{1,0:T(8,128)(2,1)S(1)} %collective-permute-done.8), kind=kLoop, calls=%fused_computation | loop fusion | flops 589824 | bytes 1572864 | tf_op jit(solution)/shard_map/convert_element_type | solution.py:410
  (9 shorter events, 0.0 us)
Async XLA Ops:
  37.5 30.2 %all-to-all-start.1 = ((bf16[16,96,128]{2,1,0:T(8,128)(2,1)}), bf16[16,96,128]{2,1,0:T(8,128)(2,1)S(1)}, u32[]{:S(2)}, u32[]{:S(2)}) async-start(bf16[16,96,128]{2,1,0:T(8,128)(2,1)} %get-tuple-element.15), calls=%async_computation.1 | async-start | bytes 786432 | tf_op jit(solution)/shard_map/all_to_all | solution.py:351
  41.0 6.0 %collective-permute-start.1 = (bf16[16,32,128]{2,1,0:T(8,128)(2,1)S(1)}, bf16[16,32,128]{2,1,0:T(8,128)(2,1)S(1)}, u32[]{:S(2)}, u32[]{:S(2)}) collective-permute-start(bf16[16,32,128]{2,1,0:T(8,128)(2,1)S(1)} %slice.9.rest_0_), channel_id=1, source_target_pairs={{0,96},{2,98},{4,100},{6,102},{8,104},{10,106},{12,108},{14,110},{... | collective-permute-start | bytes 393224 | tf_op jit(solution)/shard_map/ppermute | solution.py:365
  44.6 23.2 %collective-permute-start = (bf16[8,192,128]{2,1,0:T(8,128)(2,1)}, bf16[8,192,128]{2,1,0:T(8,128)(2,1)S(1)}, u32[]{:S(2)}, u32[]{:S(2)}) collective-permute-start(bf16[8,192,128]{2,1,0:T(8,128)(2,1)} %slice.8), channel_id=1, source_target_pairs={{0,32},{2,34},{4,36},{6,38},{8,40},{10,42},{12,44},{14,46},{16,48}... | collective-permute-start | bytes 1179656 | tf_op jit(solution)/shard_map/ppermute | solution.py:355
  46.5 5.2 %collective-permute-start.4 = (bf16[16,32,128]{2,1,0:T(8,128)(2,1)S(1)}, bf16[16,32,128]{2,1,0:T(8,128)(2,1)S(1)}, u32[]{:S(2)}, u32[]{:S(2)}) collective-permute-start(bf16[16,32,128]{2,1,0:T(8,128)(2,1)S(1)} %slice.9.rest_0_), channel_id=1, source_target_pairs={{0,128},{2,130},{4,132},{6,134},{8,136},{10,138},{12,140},{14,142}... | collective-permute-start | bytes 393224 | tf_op jit(solution)/shard_map/ppermute | solution.py:365
  46.6 16.1 %collective-permute-start.3 = (bf16[16,32,128]{2,1,0:T(8,128)(2,1)S(1)}, bf16[16,32,128]{2,1,0:T(8,128)(2,1)S(1)}, u32[]{:S(2)}, u32[]{:S(2)}) collective-permute-start(bf16[16,32,128]{2,1,0:T(8,128)(2,1)S(1)} %slice.9.rest_0_), channel_id=1, source_target_pairs={{0,32},{2,34},{4,36},{6,38},{8,40},{10,42},{12,44},{14,46},{16,48}... | collective-permute-start | bytes 393224 | tf_op jit(solution)/shard_map/ppermute | solution.py:365
  47.0 15.7 %collective-permute-start.2 = (bf16[16,32,128]{2,1,0:T(8,128)(2,1)S(1)}, bf16[16,32,128]{2,1,0:T(8,128)(2,1)S(1)}, u32[]{:S(2)}, u32[]{:S(2)}) collective-permute-start(bf16[16,32,128]{2,1,0:T(8,128)(2,1)S(1)} %collective-permute-done.1.rest_1_), channel_id=1, source_target_pairs={{0,96},{2,98},{4,100},{6,102},{8,104},{10,106},{12,108},{14,110},{... | collective-permute-start | bytes 393224 | tf_op jit(solution)/shard_map/ppermute | solution.py:365
  51.7 16.0 %collective-permute-start.5 = (bf16[16,32,128]{2,1,0:T(8,128)(2,1)S(1)}, bf16[16,32,128]{2,1,0:T(8,128)(2,1)S(1)}, u32[]{:S(2)}, u32[]{:S(2)}) collective-permute-start(bf16[16,32,128]{2,1,0:T(8,128)(2,1)S(1)} %collective-permute-done.4.rest_4_), channel_id=1, source_target_pairs={{0,96},{2,98},{4,100},{6,102},{8,104},{10,106},{12,108},{14,110},{... | collective-permute-start | bytes 393224 | tf_op jit(solution)/shard_map/ppermute | solution.py:365
  62.7 5.1 %collective-permute-start.7 = (bf16[16,32,128]{2,1,0:T(8,128)(2,1)S(1)}, bf16[16,32,128]{2,1,0:T(8,128)(2,1)S(1)}, u32[]{:S(2)}, u32[]{:S(2)}) collective-permute-start(bf16[16,32,128]{2,1,0:T(8,128)(2,1)S(1)} %collective-permute-done.3.rest_3_), channel_id=1, source_target_pairs={{0,128},{2,130},{4,132},{6,134},{8,136},{10,138},{12,140},{14,142}... | collective-permute-start | bytes 393224 | tf_op jit(solution)/shard_map/ppermute | solution.py:365
  62.7 6.8 %collective-permute-start.6 = (bf16[16,32,128]{2,1,0:T(8,128)(2,1)S(1)}, bf16[16,32,128]{2,1,0:T(8,128)(2,1)S(1)}, u32[]{:S(2)}, u32[]{:S(2)}) collective-permute-start(bf16[16,32,128]{2,1,0:T(8,128)(2,1)S(1)} %collective-permute-done.2.rest_2_), channel_id=1, source_target_pairs={{0,128},{2,130},{4,132},{6,134},{8,136},{10,138},{12,140},{14,142}... | collective-permute-start | bytes 393224 | tf_op jit(solution)/shard_map/ppermute | solution.py:365
  64.1 0.7 copy-start.3
  64.8 0.7 copy-start.4
  69.5 0.7 copy-start.2
  89.1 22.7 %all-to-all-start.2 = ((bf16[16,96,128]{2,1,0:T(8,128)(2,1)}), bf16[16,96,128]{2,1,0:T(8,128)(2,1)S(1)}, u32[]{:S(2)}, u32[]{:S(2)}) async-start(bf16[16,96,128]{2,1,0:T(8,128)(2,1)} %attend.1), calls=%async_computation.2 | async-start | bytes 786432 | tf_op jit(solution)/shard_map/all_to_all | solution.py:351
  111.8 7.3 %copy-start.1 = (bf16[16,96,128]{2,1,0:T(8,128)(2,1)}, bf16[16,96,128]{2,1,0:T(8,128)(2,1)S(1)}, u32[]{:S(2)}) copy-start(bf16[16,96,128]{2,1,0:T(8,128)(2,1)S(1)} %all-to-all-done.2) | copy-start | bytes 1179652
  111.8 3.8 %copy-start = (bf16[1536,3072]{1,0:T(8,128)(2,1)S(1)}, bf16[1536,3072]{1,0:T(8,128)(2,1)}, u32[]{:S(2)}) copy-start(bf16[1536,3072]{1,0:T(8,128)(2,1)} %w_ref.3) | copy-start | bytes 28311556
  117.2 12.1 %collective-permute-start.8 = (bf16[1536,128]{1,0:T(8,128)(2,1)S(1)}, bf16[1536,128]{1,0:T(8,128)(2,1)S(1)}, u32[]{:S(2)}, u32[]{:S(2)}) collective-permute-start(bf16[1536,128]{1,0:T(8,128)(2,1)S(1)} %project_here.1), channel_id=1, source_target_pairs={{0,1},{1,0},{2,3},{3,2},{4,5},{5,4},{6,7},{7,6},{8,9},{9,8},{10,11... | collective-permute-start | bytes 1179656 | tf_op jit(solution)/shard_map/ppermute | solution.py:408

commit v3 on v2

v3 whole, which is shorter than its diff:
```python
import functools
import math

import jax
import jax.numpy as jnp
from jax import lax
from jax.experimental import pallas as pl
from jax.experimental.pallas import tpu as pltpu
from jax.sharding import PartitionSpec as P

HD = 96
W = 1024
SINKS = 4
G = 2
RING = 16
BLK = 128
QB = 256
CH = 256
LANES = 128
FAR = 1 << 28
LOW = -1e30
VMEM_LIMIT = 24 << 20


def pack_kernel(k_ref, v_ref, ck_ref, cv_ref, out_ref):
    heads = k_ref.shape[1] // HD
    for which, ref in enumerate((k_ref, v_ref)):
        turned = ref[...].T
        for p in range(heads):
            out_ref[p, which * HD : (which + 1) * HD, :] = turned[p * HD : (p + 1) * HD, :]
    rows = ck_ref.shape[0]
    fill = jnp.zeros((rows, LANES - HD), ck_ref.dtype)
    for which, ref in enumerate((ck_ref, cv_ref)):
        for p in range(heads):
            piece = jnp.concatenate([ref[:, p * HD : (p + 1) * HD], fill], axis=1)
            base = 2 * HD + which * rows
            out_ref[p, base : base + rows, :] = piece


def pack_query_kernel(head, q_ref, sk_ref, sv_ref, query_ref, sink_ref):
    turned = q_ref[...].T
    for p in range(q_ref.shape[1] // HD):
        query_ref[p] = turned[p * HD : (p + 1) * HD, :]
    width = sk_ref.shape[1]
    column = lax.broadcasted_iota(jnp.int32, (width, LANES), 0)
    lane = lax.broadcasted_iota(jnp.int32, (width, LANES), 1)
    pick = ((column == head[0] * HD + lane) & (lane < HD)).astype(jnp.float32).astype(jnp.bfloat16)
    for which, ref in enumerate((sk_ref, sv_ref)):
        piece = jnp.dot(ref[...], pick, preferred_element_type=jnp.float32)
        piece = jnp.concatenate([piece, jnp.zeros_like(piece)], axis=0)
        sink_ref[which * 16 : (which + 1) * 16, :] = piece.astype(jnp.bfloat16)


def gather_facts(place, lengths, groups, need, blocks):
    base = place[0] * RING * BLK
    own = RING * BLK
    for b in range((1 + G) * blocks):
        need[b] = FAR

    def one_request(r, carry):
        start, start_col, group_col = carry
        length = lengths[r]
        group = groups[r]
        first = jnp.where(start < base, 0, (start - base) // QB)
        last = jnp.minimum((start + length - 1 - base) // QB, blocks - 1)

        def mark(b, _):
            need[b] = jnp.minimum(need[b], start)
            offset = jnp.maximum(base + b * QB - start, 0)
            at = (1 + group) * blocks + b
            need[at] = jnp.minimum(need[at], offset)
            return 0

        @pl.when((start < base + own) & (start + length > base))
        def _():
            lax.fori_loop(first, last + 1, mark, 0)

        row = lax.broadcasted_iota(jnp.int32, start_col.shape, 0)
        start_col = jnp.where(row == r, start, start_col)
        group_col = jnp.where(row == r, group, group_col)
        return (start + length, start_col, group_col)

    reqs = lengths.shape[0]
    column = jnp.zeros((reqs, QB), jnp.int32)
    _, start_col, group_col = lax.fori_loop(0, reqs, one_request, (jnp.int32(0), column, column))
    return base, start_col, group_col


def query_facts(index, start_col, group_col):
    begun = start_col <= index
    start_q = jnp.max(jnp.where(begun, start_col, 0), axis=0, keepdims=True)
    here = begun & (start_col == start_q)
    group_q = jnp.max(jnp.where(here, group_col, 0), axis=0, keepdims=True)
    return jnp.maximum(start_q, index - (W - 1)), index - start_q, group_q


def turn(piece):
    pad = jnp.zeros((LANES - HD, BLK), jnp.bfloat16)
    return jnp.concatenate([piece, pad], axis=0).T


def query_block(query_ref, b):
    q_t = jnp.concatenate([query_ref[2 * b], query_ref[2 * b + 1]], axis=1)
    return jnp.concatenate([q_t, jnp.zeros((LANES - HD, QB), jnp.bfloat16)], axis=0)


def values(val_ref, at):
    slot = at // BLK
    return jnp.concatenate([val_ref[slot], val_ref[slot + 1]], axis=1)


def dot(a, b):
    return jnp.dot(a, b, preferred_element_type=jnp.float32)


FACTOR = (1.0 / math.sqrt(HD)) * math.log2(math.e)


def prep_kernel(place, lengths, groups, own_ref, key_ref, low_ref, need):
    for j in range(RING):
        key_ref[j * BLK : (j + 1) * BLK, :] = turn(own_ref[j, 0:HD, :])
    own = RING * BLK
    blocks = own // QB
    cache_at = own
    base, start_col, group_col = gather_facts(place, lengths, groups, need, blocks)
    lane = lax.broadcasted_iota(jnp.int32, (1, QB), 1)
    for b in range(blocks):
        index = base + b * QB + lane
        low_q, offset, group_q = query_facts(index, start_col, group_col)
        low_ref[b, 0:1, :] = low_q - base
        for g in range(G):
            low_ref[b, 1 + g : 2 + g, :] = jnp.where(
                group_q == g, cache_at + g * W + offset + 1, FAR
            )
        low_ref[b, 1 + G : 2 + G, :] = jnp.full((1, QB), FAR, jnp.int32)
        low_ref[b, 2 + G : 3 + G, :] = group_q


def visit(total, where_is, key_ref, val_ref, low_of, q_t, state):
    row_iota = lax.broadcasted_iota(jnp.int32, (CH, QB), 0)

    def step(j, state):
        top, den, acc = state
        scores, ats = [], []
        for u in range(2):
            at, kind = where_is(2 * j + u)
            s = dot(key_ref[pl.ds(at, CH), :], q_t)
            scores.append(jnp.where(row_iota >= low_of(kind) - at, s, LOW))
            ats.append(at)
        new = jnp.maximum(
            jnp.max(scores[0], axis=0, keepdims=True), jnp.max(scores[1], axis=0, keepdims=True)
        )
        new = jnp.maximum(top, new)
        fade = jnp.exp2((top - new) * FACTOR)
        den = den * fade
        ps = []
        for u in range(2):
            p = jnp.exp2((scores[u] - new) * FACTOR)
            den = den + jnp.sum(p, axis=0, keepdims=True)
            ps.append(p.astype(jnp.bfloat16))
        vals = jnp.concatenate([values(val_ref, at) for at in ats], axis=1)
        acc = acc * fade + dot(vals, jnp.concatenate(ps, axis=0))
        return (new, den, acc)

    return lax.fori_loop(0, (total + 1) // 2, step, state)


def attend_kernel(
    place, need, low_ref, sink_ref, query_ref, own_ref, turned_ref, *rest, rings
):
    caches = rest[:rings]
    upper_ref, stat_ref, acc_ref, key_ref, val_ref = rest[rings:]
    ring = place[0]
    base = ring * RING * BLK
    own = RING * BLK
    blocks = own // QB
    key_ref[0:own, :] = turned_ref[...]
    for j in range(RING):
        val_ref[j] = own_ref[j, HD : 2 * HD, :]
    rows = RING * 16
    for k in range(rings):
        source = lax.rem(lax.rem(ring, 4) + k % 4, 4) + 4 * lax.rem(ring // 4 + k // 4, 2)
        piece = caches[k][...]
        at = pl.multiple_of(own + source * rows, rows)
        key_ref[pl.ds(at, rows), :] = piece[:, 0:16, :].reshape(rows, LANES)
        turned = piece[:, 16:32, :].reshape(rows, LANES).T
        for half in range(rows // BLK):
            val_ref[at // BLK + half] = turned[0:HD, half * BLK : (half + 1) * BLK]
    lane = lax.broadcasted_iota(jnp.int32, (1, QB), 1)
    row_iota = lax.broadcasted_iota(jnp.int32, (CH, QB), 0)
    sink_row = lax.broadcasted_iota(jnp.int32, (16, QB), 0)
    sink_v = sink_ref[16:32, :].T[0:HD, :]

    def one_block(b, _):
        low_suffix = low_ref[b, 0:1, :]
        group_q = low_ref[b, 2 + G : 3 + G, :]
        q_t = query_block(query_ref, b)
        at0 = pl.multiple_of(b * QB, CH)
        s_d = dot(key_ref[pl.ds(at0, CH), :], q_t)
        s_d = jnp.where((row_iota >= low_suffix - at0) & (row_iota <= lane), s_d, LOW)
        s_s = dot(sink_ref[0:16, :], q_t)
        s_s = jnp.where((sink_row // SINKS == group_q) & (sink_row < G * SINKS), s_s, LOW)
        top = jnp.maximum(jnp.max(s_d, axis=0, keepdims=True), jnp.max(s_s, axis=0, keepdims=True))
        p_d = jnp.exp2((s_d - top) * FACTOR)
        p_s = jnp.exp2((s_s - top) * FACTOR)
        den = jnp.sum(p_d, axis=0, keepdims=True) + jnp.sum(p_s, axis=0, keepdims=True)
        acc = dot(values(val_ref, at0), p_d.astype(jnp.bfloat16))
        acc = acc + dot(sink_v, p_s.astype(jnp.bfloat16))

        first = jnp.maximum(jnp.maximum(need[b] - base, b * QB - (W - 1)), 0) // CH
        n_suffix = b - first
        c0 = [jnp.minimum((need[(1 + g) * blocks + b] + 1) // CH, W // CH) for g in range(G)]
        n0, n1 = [W // CH - c for c in c0]
        total = n_suffix + n0 + n1

        def where_is(j):
            in0 = j - n_suffix
            in1 = in0 - n0
            at = jnp.where(
                in0 < 0,
                (first + j) * CH,
                jnp.where(
                    in1 < 0,
                    own + (c0[0] + in0) * CH,
                    jnp.where(j < total, own + W + (c0[1] + in1) * CH, 0),
                ),
            )
            kind = jnp.where(in0 < 0, 0, jnp.where(in1 < 0, 1, jnp.where(j < total, 2, 3)))
            return pl.multiple_of(at, CH), kind

        def low_of(kind):
            return low_ref[b, pl.ds(kind, 1), :]

        top, den, acc = visit(total, where_is, key_ref, val_ref, low_of, q_t, (top, den, acc))

        @pl.when(b < blocks // 2)
        def _():
            stat_ref[b, 0:1, :] = top
            stat_ref[b, 1:2, :] = den
            acc_ref[b] = acc

        @pl.when(b >= blocks // 2)
        def _():
            done = (acc / den).astype(jnp.bfloat16)
            upper_ref[2 * b - RING // 2] = done[:, 0:BLK]
            upper_ref[2 * b + 1 - RING // 2] = done[:, BLK:QB]

        return 0

    lax.fori_loop(0, blocks, one_block, 0)


def window_kernel(
    place, need, low_ref, query_ref, win_ref, upper_ref, stat_ref, acc_ref, out_ref,
    key_ref, val_ref,
):
    base = place[0] * RING * BLK
    blocks = RING * BLK // QB
    for j in range(RING // 2):
        key_ref[j * BLK : (j + 1) * BLK, :] = turn(win_ref[j, 0:HD, :])
        val_ref[j] = win_ref[j, HD : 2 * HD, :]
        out_ref[RING // 2 + j] = upper_ref[j]

    def one_block(b, _):
        q_t = query_block(query_ref, b)
        first = jnp.maximum(need[b] - base, b * QB - (W - 1)) + W
        first = jnp.minimum(first // CH, W // CH)
        total = W // CH - first

        def where_is(j):
            at = jnp.where(j < total, (first + j) * CH, 0)
            return pl.multiple_of(at, CH), jnp.where(j < total, 0, 1 + G)

        def low_of(kind):
            return low_ref[b, pl.ds(kind, 1), :] + jnp.where(kind == 0, W, 0)

        state = (stat_ref[b, 0:1, :], stat_ref[b, 1:2, :], acc_ref[b])
        _, den, acc = visit(total, where_is, key_ref, val_ref, low_of, q_t, state)
        done = (acc / den).astype(jnp.bfloat16)
        out_ref[2 * b] = done[:, 0:BLK]
        out_ref[2 * b + 1] = done[:, BLK:QB]
        return 0

    lax.fori_loop(0, blocks // 2, one_block, 0)


def project_kernel(side, attn_ref, w_ref, out_ref, half_ref, sum_ref, arrived):
    features = half_ref.shape[1]
    columns = pl.ds(pl.multiple_of(side[0] * features, features), features)
    parts = arrived.shape[0]
    tall = half_ref.shape[0] // parts
    loads = []
    for n in range(parts):
        rows = pl.ds(n * tall, tall)
        loads.append(
            pltpu.make_async_copy(w_ref.at[rows, columns], half_ref.at[rows, :], arrived.at[n])
        )
    for load in loads:
        load.start()
    turned = attn_ref[...].T
    for n in range(parts):
        loads[n].wait()
        at = slice(n * tall, (n + 1) * tall)
        part = dot(turned[:, at], half_ref[at, :])
        if n == 0:
            sum_ref[...] = part
        elif n < parts - 1:
            sum_ref[...] += part
        else:
            out_ref[...] = (sum_ref[...] + part).T.astype(out_ref.dtype)


def project(side, attn_t, w_out, dtype):
    width, rows = attn_t.shape
    features = w_out.shape[1] // 2
    return pl.pallas_call(
        project_kernel,
        out_shape=jax.ShapeDtypeStruct((features, rows), dtype),
        in_specs=[smem(), vmem(), pl.BlockSpec(memory_space=pltpu.HBM)],
        out_specs=vmem(),
        scratch_shapes=[
            pltpu.VMEM((width, features), jnp.bfloat16),
            pltpu.VMEM((rows, features), jnp.float32),
            pltpu.SemaphoreType.DMA((6,)),
        ],
        cost_estimate=pl.CostEstimate(
            flops=2 * width * features * rows,
            bytes_accessed=2 * width * features,
            transcendentals=0,
        ),
        compiler_params=pltpu.CompilerParams(vmem_limit_bytes=50 << 20),
        name="project",
    )(side.reshape(1), attn_t, w_out)


def vmem():
    return pl.BlockSpec(memory_space=pltpu.VMEM)


def smem():
    return pl.BlockSpec(memory_space=pltpu.SMEM)


def shards(
    queries, keys, values, cache_k, cache_v, sink_k, sink_v, suffix_lengths, request_group, w_out
):
    rows, width = queries.shape
    heads = width // HD
    seq = lax.axis_size("seq")
    rings = seq // RING
    device = lax.axis_index("seq")
    half = lax.axis_index("head")
    packed = pl.pallas_call(
        pack_kernel,
        out_shape=jax.ShapeDtypeStruct((heads, 2 * HD + 32, LANES), jnp.bfloat16),
        in_specs=[vmem()] * 4,
        out_specs=vmem(),
        name="pack",
    )(keys, values, cache_k, cache_v)
    packed_q, sinks = pl.pallas_call(
        pack_query_kernel,
        out_shape=(
            jax.ShapeDtypeStruct((heads, HD, LANES), jnp.bfloat16),
            jax.ShapeDtypeStruct((32, LANES), jnp.bfloat16),
        ),
        in_specs=[smem()] + [vmem()] * 3,
        out_specs=(vmem(), vmem()),
        cost_estimate=pl.CostEstimate(flops=1 << 20, bytes_accessed=1 << 21, transcendentals=0),
        name="pack_query",
    )((device % RING).reshape(1), queries, sink_k, sink_v)
    members = [[r * RING + i for i in range(RING)] for r in range(rings)]

    def trade(array, groups):
        return lax.all_to_all(array, "seq", 0, 0, axis_index_groups=groups, tiled=True)

    mine = trade(packed, members)
    mine_q = trade(packed_q, members)
    cache = mine[:, 2 * HD :, :]

    def send(array, dx, dy):
        pairs = []
        for r in range(rings):
            to = (r % 4 + dy) % 4 + 4 * ((r // 4 + dx) % 2)
            pairs += [(r * RING + i, to * RING + i) for i in range(RING)]
        return lax.ppermute(array, "seq", pairs)

    near_y = send(cache, 0, 3)
    near_x = send(cache, 1, 0)
    back_y = send(cache, 0, 1)
    far_y = send(near_y, 0, 3)
    near_xy = send(near_x, 0, 3)
    back_xy = send(back_y, 1, 0)
    far_xy = send(far_y, 1, 0)
    window = lax.ppermute(
        mine[RING // 2 :, : 2 * HD, :], "seq", [(s, s + RING) for s in range(seq - RING)]
    )
    caches = [cache, near_y, far_y, back_y, near_x, near_xy, far_xy, back_xy]
    own = RING * BLK
    blocks = own // QB
    place = (device // RING).reshape(1)
    turned, lows, need = pl.pallas_call(
        prep_kernel,
        out_shape=(
            jax.ShapeDtypeStruct((own, LANES), jnp.bfloat16),
            jax.ShapeDtypeStruct((blocks, 8, QB), jnp.int32),
            jax.ShapeDtypeStruct(((1 + G) * blocks,), jnp.int32),
        ),
        in_specs=[smem()] * 3 + [vmem()],
        out_specs=(vmem(), vmem(), smem()),
        cost_estimate=pl.CostEstimate(
            flops=1 << 20, bytes_accessed=1 << 22, transcendentals=0
        ),
        compiler_params=pltpu.CompilerParams(vmem_limit_bytes=VMEM_LIMIT),
        name="prep",
    )(place, suffix_lengths, request_group, mine)
    upper, stats, sums = pl.pallas_call(
        functools.partial(attend_kernel, rings=rings),
        out_shape=(
            jax.ShapeDtypeStruct((RING // 2, HD, BLK), jnp.bfloat16),
            jax.ShapeDtypeStruct((blocks // 2, 8, QB), jnp.float32),
            jax.ShapeDtypeStruct((blocks // 2, HD, QB), jnp.float32),
        ),
        in_specs=[smem()] * 2 + [vmem()] * (5 + rings),
        out_specs=(vmem(), vmem(), vmem()),
        scratch_shapes=[
            pltpu.VMEM((own + G * W, LANES), jnp.bfloat16),
            pltpu.VMEM(((own + G * W) // BLK, HD, BLK), jnp.bfloat16),
        ],
        cost_estimate=pl.CostEstimate(
            flops=own * 2 * W * HD * 4, bytes_accessed=1 << 22, transcendentals=own * 2 * W
        ),
        compiler_params=pltpu.CompilerParams(vmem_limit_bytes=VMEM_LIMIT),
        name="attend",
    )(place, need, lows, sinks, mine_q, mine, turned, *caches)
    attn = pl.pallas_call(
        window_kernel,
        out_shape=jax.ShapeDtypeStruct((RING, HD, BLK), jnp.bfloat16),
        in_specs=[smem()] * 2 + [vmem()] * 6,
        out_specs=vmem(),
        scratch_shapes=[
            pltpu.VMEM((W, LANES), jnp.bfloat16),
            pltpu.VMEM((W // BLK, HD, BLK), jnp.bfloat16),
        ],
        compiler_params=pltpu.CompilerParams(vmem_limit_bytes=VMEM_LIMIT),
        name="window",
    )(place, need, lows, mine_q, window, upper, stats, sums)
    attn_t = trade(attn, members).reshape(width, rows)
    give = project(1 - half, attn_t, w_out, jnp.bfloat16)
    got = lax.ppermute(give, "head", [(0, 1), (1, 0)])
    keep = project(half, attn_t, w_out, jnp.float32)
    return (keep + got.astype(jnp.float32)).astype(jnp.bfloat16)


def solution(mesh):
    placed = (
        P("seq", "head"),
        P("seq", "head"),
        P("seq", "head"),
        P("seq", "head"),
        P("seq", "head"),
        P(None, "head"),
        P(None, "head"),
        P(),
        P(),
        P("head", None),
    )
    return jax.shard_map(
        shards, mesh=mesh, in_specs=placed, out_specs=P("head", "seq"), check_vma=False
    )
```

time: 132 us -> 126 us (0.955)
  the two profiles are of different devices: /device:TPU:3 before, /device:TPU:27 now
where the time goes in v3:
time: 126 us; the launch traced here: 125 us
  waiting for transfers between devices  58.8 us (47%)
  starting transfers between devices  31.6 us (25%)
  Pallas kernels  31.3 us (25%)
  local copies, waits for them, and re-layouts  2.8 us (2%)
    all_to_all x3, waiting for transfers between devices, trade(): lax.all_to_all(array, 'seq', 0, 0, axis_index_groups=groups, tiled=True)  37.9 us
    all_to_all x3, starting transfers between devices, trade(): lax.all_to_all(array, 'seq', 0, 0, axis_index_groups=groups, tiled=True)  20.6 us
    pallas_call x1, Pallas kernels, shards(): pl.pallas_call(functools.partial(attend_kernel, rings=rings), out_shape=(...  16.7 us
    ppermute x7, waiting for transfers between devices, send(): return lax.ppermute(array, 'seq', pairs)  13.6 us
    ppermute x7, starting transfers between devices, send(): return lax.ppermute(array, 'seq', pairs)  7.77 us
    ppermute x1, waiting for transfers between devices, shards(): got = lax.ppermute(give, 'head', [(0, 1), (1, 0)])  7.38 us
    pallas_call x2, Pallas kernels, project(): pl.pallas_call(project_kernel, out_shape=jax.ShapeDtypeStruct((features,...  5.54 us
  transfers between devices with their start and end apart: 12, of which 6 were waited for; matrix products, arithmetic and copies ran while one was open for 1% of the time, Pallas kernels for 19%

profile of v3, /device:TPU:27, one launch (start us, length us, event | category | flops | bytes accessed | tf_op | source)
XLA Modules:
  0.0 125.5 jit_solution(6985783654836320544)
XLA Ops:
  0.0 2.4 %pack.1 = bf16[16,224,128]{2,1,0:T(8,128)(2,1)} custom-call(bf16[128,1536]{1,0:T(8,128)(2,1)} %k_ref.1, bf16[128,1536]{1,0:T(8,128)(2,1)} %v_ref.1, bf16[16,1536]{1,0:T(8,128)(2,1)} %ck_ref.1, bf16[16,1536]{1,0:T(8,128)(2,1)} %cv_ref.1), custom_call_target="tpu_custom_call" | custom-call | tf_op jit(solution)/shard_map/pack/pallas_call | solution.py:353
  2.4 9.2 %all-to-all-start = ((bf16[16,224,128]{2,1,0:T(8,128)(2,1)}), bf16[16,224,128]{2,1,0:T(8,128)(2,1)S(1)}, u32[]{:S(2)}, u32[]{:S(2)}) async-start(bf16[16,224,128]{2,1,0:T(8,128)(2,1)} %pack.1), calls=%async_computation | async-start | bytes 1835008 | tf_op jit(solution)/shard_map/all_to_all | solution.py:374
  11.5 2.0 %pack_query.1 = (bf16[16,96,128]{2,1,0:T(8,128)(2,1)}, bf16[32,128]{1,0:T(8,128)(2,1)}) custom-call(s32[1]{0:T(128)} %bitcast.2.head, bf16[128,1536]{1,0:T(8,128)(2,1)} %q_ref.1, bf16[8,1536]{1,0:T(8,128)(2,1)} %sk_ref.1, bf16[8,1536]{1,0:T(8,128)(2,1)} %sv_ref.1), custom_call_target="tpu_custom_call" | custom-call | flops 1048576 | bytes 2097152 | tf_op jit(solution)/shard_map/pack_query/pallas_call | solution.py:360
  13.5 23.4 %all-to-all-done.own_ref = bf16[16,224,128]{2,1,0:T(8,128)(2,1)S(1)} async-done(((bf16[16,224,128]{2,1,0:T(8,128)(2,1)}), bf16[16,224,128]{2,1,0:T(8,128)(2,1)S(1)}, u32[]{:S(2)}, u32[]{:S(2)}) %all-to-all-start) | async-done | bytes 917536 | tf_op jit(solution)/shard_map/all_to_all | solution.py:374
  36.9 3.5 %all-to-all-start.1 = ((bf16[16,96,128]{2,1,0:T(8,128)(2,1)}), bf16[16,96,128]{2,1,0:T(8,128)(2,1)S(1)}, u32[]{:S(2)}, u32[]{:S(2)}) async-start(bf16[16,96,128]{2,1,0:T(8,128)(2,1)} %get-tuple-element.15), calls=%async_computation.1 | async-start | bytes 786432 | tf_op jit(solution)/shard_map/all_to_all | solution.py:374
  40.4 0.5 collective-permute-start.1
  40.9 0.3 collective-permute-start.4
  41.2 2.2 %collective-permute-start.3 = (bf16[16,32,128]{2,1,0:T(8,128)(2,1)S(1)}, bf16[16,32,128]{2,1,0:T(8,128)(2,1)S(1)}, u32[]{:S(2)}, u32[]{:S(2)}) collective-permute-start(bf16[16,32,128]{2,1,0:T(8,128)(2,1)S(1)} %slice.9.rest_0_), channel_id=1, source_target_pairs={{0,32},{2,34},{4,36},{6,38},{8,40},{10,42},{12,44},{14,46},{16,48}... | collective-permute-start | bytes 393224 | tf_op jit(solution)/shard_map/ppermute | solution.py:385
  43.4 3.4 %collective-permute-done.1.rest_1_ = bf16[16,32,128]{2,1,0:T(8,128)(2,1)S(1)} collective-permute-done((bf16[16,32,128]{2,1,0:T(8,128)(2,1)S(1)}, bf16[16,32,128]{2,1,0:T(8,128)(2,1)S(1)}, u32[]{:S(2)}, u32[]{:S(2)}) %collective-permute-start.1) | collective-permute-done | bytes 131104 | tf_op jit(solution)/shard_map/ppermute | solution.py:385
  46.8 0.8 slice.8
  47.6 1.3 %collective-permute-start = (bf16[8,192,128]{2,1,0:T(8,128)(2,1)}, bf16[8,192,128]{2,1,0:T(8,128)(2,1)S(1)}, u32[]{:S(2)}, u32[]{:S(2)}) collective-permute-start(bf16[8,192,128]{2,1,0:T(8,128)(2,1)} %slice.8), channel_id=1, source_target_pairs={{0,32},{2,34},{4,36},{6,38},{8,40},{10,42},{12,44},{14,46},{16,48}... | collective-permute-start | bytes 1179656 | tf_op jit(solution)/shard_map/ppermute | solution.py:394
  48.9 0.0 collective-permute-done.4.rest_4_
  48.9 2.2 %collective-permute-start.5 = (bf16[16,32,128]{2,1,0:T(8,128)(2,1)S(1)}, bf16[16,32,128]{2,1,0:T(8,128)(2,1)S(1)}, u32[]{:S(2)}, u32[]{:S(2)}) collective-permute-start(bf16[16,32,128]{2,1,0:T(8,128)(2,1)S(1)} %collective-permute-done.4.rest_4_), channel_id=1, source_target_pairs={{0,96},{2,98},{4,100},{6,102},{8,104},{10,106},{12,108},{14,110},{... | collective-permute-start | bytes 393224 | tf_op jit(solution)/shard_map/ppermute | solution.py:385
  51.0 0.0 collective-permute-done.3.rest_3_
  51.0 2.5 %collective-permute-start.7 = (bf16[16,32,128]{2,1,0:T(8,128)(2,1)S(1)}, bf16[16,32,128]{2,1,0:T(8,128)(2,1)S(1)}, u32[]{:S(2)}, u32[]{:S(2)}) collective-permute-start(bf16[16,32,128]{2,1,0:T(8,128)(2,1)S(1)} %collective-permute-done.3.rest_3_), channel_id=1, source_target_pairs={{0,128},{2,130},{4,132},{6,134},{8,136},{10,138},{12,140},{14,142}... | collective-permute-start | bytes 393224 | tf_op jit(solution)/shard_map/ppermute | solution.py:385
  53.5 0.0 collective-permute-done.2.rest_2_
  53.5 0.1 collective-permute-start.6
  53.7 0.7 copy-done
  54.3 0.7 copy-done.1
  55.0 2.2 %prep.1 = (bf16[2048,128]{1,0:T(8,128)(2,1)S(1)}, s32[8,8,256]{2,1,0:T(8,128)S(1)}, s32[24]{0:T(128)S(1)}) custom-call(s32[1]{0:T(128)} %bitcast.1.place, s32[32]{0:T(128)S(1)} %copy-done, s32[32]{0:T(128)S(1)} %copy-done.1, bf16[16,224,128]{2,1,0:T(8,128)(2,1)S(1)} %all-to-all-done.own_ref), custom_call_target="tpu_custom_call" | custom-call | flops 1048576 | bytes 4194304 | tf_op jit(solution)/shard_map/prep/pallas_call | solution.py:401
  57.2 7.0 %collective-permute-done.7.rest_7_ = bf16[16,32,128]{2,1,0:T(8,128)(2,1)S(1)} collective-permute-done((bf16[16,32,128]{2,1,0:T(8,128)(2,1)S(1)}, bf16[16,32,128]{2,1,0:T(8,128)(2,1)S(1)}, u32[]{:S(2)}, u32[]{:S(2)}) %collective-permute-start.7) | collective-permute-done | bytes 131104 | tf_op jit(solution)/shard_map/ppermute | solution.py:385
  64.2 3.1 %collective-permute-done.6.rest_6_ = bf16[16,32,128]{2,1,0:T(8,128)(2,1)S(1)} collective-permute-done((bf16[16,32,128]{2,1,0:T(8,128)(2,1)S(1)}, bf16[16,32,128]{2,1,0:T(8,128)(2,1)S(1)}, u32[]{:S(2)}, u32[]{:S(2)}) %collective-permute-start.6) | collective-permute-done | bytes 131104 | tf_op jit(solution)/shard_map/ppermute | solution.py:385
  67.3 0.7 copy-done.2
  68.0 16.7 %attend.1 = (bf16[8,96,128]{2,1,0:T(8,128)(2,1)S(1)}, f32[4,8,256]{2,1,0:T(8,128)S(1)}, f32[4,96,256]{2,1,0:T(8,128)S(1)}) custom-call(s32[1]{0:T(128)} %bitcast.1.place, s32[24]{0:T(128)S(1)} %get-tuple-element.13.need, s32[8,8,256]{2,1,0:T(8,128)S(1)} %get-tuple-element.14.low_ref, bf16[32,128]{1,0:T(8,128)(2,1)S(1)} %copy-done.2, ...), custom_call_target="tpu_custom_call" | custom-call | flops 1610612736 | bytes 4194304 | tf_op jit(solution)/shard_map/attend/pallas_call | solution.py:416
  84.8 2.5 %window.1 = bf16[16,96,128]{2,1,0:T(8,128)(2,1)} custom-call(s32[1]{0:T(128)} %bitcast.1.place, s32[24]{0:T(128)S(1)} %get-tuple-element.13.need, s32[8,8,256]{2,1,0:T(8,128)S(1)} %get-tuple-element.14.low_ref, bf16[16,96,128]{2,1,0:T(8,128)(2,1)S(1)} %all-to-all-done.1.query_ref, bf16[8,192,128]{2,1,0:T(8,128)(2,1)S(1)} %collective-permute-done.win_ref, ...), custom_call_target="tpu_custom_call" | custom-call | tf_op jit(solution)/shard_map/window/pallas_call | solution.py:435
  87.3 8.0 %all-to-all-start.2 = ((bf16[16,96,128]{2,1,0:T(8,128)(2,1)}), bf16[16,96,128]{2,1,0:T(8,128)(2,1)S(1)}, u32[]{:S(2)}, u32[]{:S(2)}) async-start(bf16[16,96,128]{2,1,0:T(8,128)(2,1)} %window.1), calls=%async_computation.2 | async-start | bytes 786432 | tf_op jit(solution)/shard_map/all_to_all | solution.py:374
  95.3 14.5 %all-to-all-done.2 = bf16[16,96,128]{2,1,0:T(8,128)(2,1)S(1)} async-done(((bf16[16,96,128]{2,1,0:T(8,128)(2,1)}), bf16[16,96,128]{2,1,0:T(8,128)(2,1)S(1)}, u32[]{:S(2)}, u32[]{:S(2)}) %all-to-all-start.2) | async-done | bytes 393248 | tf_op jit(solution)/shard_map/all_to_all | solution.py:374
  109.8 2.7 %project.3 = bf16[1536,128]{1,0:T(8,128)(2,1)S(1)} custom-call(s32[1]{0:T(128)} %bitcast.4.side, bf16[1536,128]{1,0:T(8,128)(2,1)S(1)} %bitcast.5, bf16[1536,3072]{1,0:T(8,128)(2,1)} %w_ref.3), custom_call_target="tpu_custom_call" | custom-call | flops 603979776 | bytes 4718592 | tf_op jit(solution)/shard_map/project/pallas_call | solution.py:316
  112.5 1.9 %collective-permute-start.8 = (bf16[1536,128]{1,0:T(8,128)(2,1)S(1)}, bf16[1536,128]{1,0:T(8,128)(2,1)S(1)}, u32[]{:S(2)}, u32[]{:S(2)}) collective-permute-start(bf16[1536,128]{1,0:T(8,128)(2,1)S(1)} %project.3), channel_id=1, source_target_pairs={{0,1},{1,0},{2,3},{3,2},{4,5},{5,4},{6,7},{7,6},{8,9},{9,8},{10,11... | collective-permute-start | bytes 1179656 | tf_op jit(solution)/shard_map/ppermute | solution.py:449
  114.4 2.8 %project.2 = f32[1536,128]{1,0:T(8,128)S(1)} custom-call(s32[1]{0:T(128)} %bitcast.side, bf16[1536,128]{1,0:T(8,128)(2,1)S(1)} %bitcast.6, bf16[1536,3072]{1,0:T(8,128)(2,1)} %w_ref.3), custom_call_target="tpu_custom_call" | custom-call | flops 603979776 | bytes 4718592 | tf_op jit(solution)/shard_map/project/pallas_call | solution.py:316
  117.3 7.4 %collective-permute-done.8 = bf16[1536,128]{1,0:T(8,128)(2,1)S(1)} collective-permute-done((bf16[1536,128]{1,0:T(8,128)(2,1)S(1)}, bf16[1536,128]{1,0:T(8,128)(2,1)S(1)}, u32[]{:S(2)}, u32[]{:S(2)}) %collective-permute-start.8) | collective-permute-done | bytes 393248 | tf_op jit(solution)/shard_map/ppermute | solution.py:449
  124.6 0.8 add_convert_fusion
  (8 shorter events, 0.0 us)
Async XLA Ops:
  2.4 34.5 %all-to-all-start = ((bf16[16,224,128]{2,1,0:T(8,128)(2,1)}), bf16[16,224,128]{2,1,0:T(8,128)(2,1)S(1)}, u32[]{:S(2)}, u32[]{:S(2)}) async-start(bf16[16,224,128]{2,1,0:T(8,128)(2,1)} %pack.1), calls=%async_computation | async-start | bytes 1835008 | tf_op jit(solution)/shard_map/all_to_all | solution.py:374
  36.9 20.3 %all-to-all-start.1 = ((bf16[16,96,128]{2,1,0:T(8,128)(2,1)}), bf16[16,96,128]{2,1,0:T(8,128)(2,1)S(1)}, u32[]{:S(2)}, u32[]{:S(2)}) async-start(bf16[16,96,128]{2,1,0:T(8,128)(2,1)} %get-tuple-element.15), calls=%async_computation.1 | async-start | bytes 786432 | tf_op jit(solution)/shard_map/all_to_all | solution.py:374
  40.4 6.4 %collective-permute-start.1 = (bf16[16,32,128]{2,1,0:T(8,128)(2,1)S(1)}, bf16[16,32,128]{2,1,0:T(8,128)(2,1)S(1)}, u32[]{:S(2)}, u32[]{:S(2)}) collective-permute-start(bf16[16,32,128]{2,1,0:T(8,128)(2,1)S(1)} %slice.9.rest_0_), channel_id=1, source_target_pairs={{0,96},{2,98},{4,100},{6,102},{8,104},{10,106},{12,108},{14,110},{... | collective-permute-start | bytes 393224 | tf_op jit(solution)/shard_map/ppermute | solution.py:385
  40.9 8.0 %collective-permute-start.4 = (bf16[16,32,128]{2,1,0:T(8,128)(2,1)S(1)}, bf16[16,32,128]{2,1,0:T(8,128)(2,1)S(1)}, u32[]{:S(2)}, u32[]{:S(2)}) collective-permute-start(bf16[16,32,128]{2,1,0:T(8,128)(2,1)S(1)} %slice.9.rest_0_), channel_id=1, source_target_pairs={{0,128},{2,130},{4,132},{6,134},{8,136},{10,138},{12,140},{14,142}... | collective-permute-start | bytes 393224 | tf_op jit(solution)/shard_map/ppermute | solution.py:385
  41.2 9.9 %collective-permute-start.3 = (bf16[16,32,128]{2,1,0:T(8,128)(2,1)S(1)}, bf16[16,32,128]{2,1,0:T(8,128)(2,1)S(1)}, u32[]{:S(2)}, u32[]{:S(2)}) collective-permute-start(bf16[16,32,128]{2,1,0:T(8,128)(2,1)S(1)} %slice.9.rest_0_), channel_id=1, source_target_pairs={{0,32},{2,34},{4,36},{6,38},{8,40},{10,42},{12,44},{14,46},{16,48}... | collective-permute-start | bytes 393224 | tf_op jit(solution)/shard_map/ppermute | solution.py:385
  46.8 6.7 %collective-permute-start.2 = (bf16[16,32,128]{2,1,0:T(8,128)(2,1)S(1)}, bf16[16,32,128]{2,1,0:T(8,128)(2,1)S(1)}, u32[]{:S(2)}, u32[]{:S(2)}) collective-permute-start(bf16[16,32,128]{2,1,0:T(8,128)(2,1)S(1)} %collective-permute-done.1.rest_1_), channel_id=1, source_target_pairs={{0,96},{2,98},{4,100},{6,102},{8,104},{10,106},{12,108},{14,110},{... | collective-permute-start | bytes 393224 | tf_op jit(solution)/shard_map/ppermute | solution.py:385
  47.6 37.2 %collective-permute-start = (bf16[8,192,128]{2,1,0:T(8,128)(2,1)}, bf16[8,192,128]{2,1,0:T(8,128)(2,1)S(1)}, u32[]{:S(2)}, u32[]{:S(2)}) collective-permute-start(bf16[8,192,128]{2,1,0:T(8,128)(2,1)} %slice.8), channel_id=1, source_target_pairs={{0,32},{2,34},{4,36},{6,38},{8,40},{10,42},{12,44},{14,46},{16,48}... | collective-permute-start | bytes 1179656 | tf_op jit(solution)/shard_map/ppermute | solution.py:394
  48.9 8.3 %collective-permute-start.5 = (bf16[16,32,128]{2,1,0:T(8,128)(2,1)S(1)}, bf16[16,32,128]{2,1,0:T(8,128)(2,1)S(1)}, u32[]{:S(2)}, u32[]{:S(2)}) collective-permute-start(bf16[16,32,128]{2,1,0:T(8,128)(2,1)S(1)} %collective-permute-done.4.rest_4_), channel_id=1, source_target_pairs={{0,96},{2,98},{4,100},{6,102},{8,104},{10,106},{12,108},{14,110},{... | collective-permute-start | bytes 393224 | tf_op jit(solution)/shard_map/ppermute | solution.py:385
  51.0 13.2 %collective-permute-start.7 = (bf16[16,32,128]{2,1,0:T(8,128)(2,1)S(1)}, bf16[16,32,128]{2,1,0:T(8,128)(2,1)S(1)}, u32[]{:S(2)}, u32[]{:S(2)}) collective-permute-start(bf16[16,32,128]{2,1,0:T(8,128)(2,1)S(1)} %collective-permute-done.3.rest_3_), channel_id=1, source_target_pairs={{0,128},{2,130},{4,132},{6,134},{8,136},{10,138},{12,140},{14,142}... | collective-permute-start | bytes 393224 | tf_op jit(solution)/shard_map/ppermute | solution.py:385
  53.5 13.8 %collective-permute-start.6 = (bf16[16,32,128]{2,1,0:T(8,128)(2,1)S(1)}, bf16[16,32,128]{2,1,0:T(8,128)(2,1)S(1)}, u32[]{:S(2)}, u32[]{:S(2)}) collective-permute-start(bf16[16,32,128]{2,1,0:T(8,128)(2,1)S(1)} %collective-permute-done.2.rest_2_), channel_id=1, source_target_pairs={{0,128},{2,130},{4,132},{6,134},{8,136},{10,138},{12,140},{14,142}... | collective-permute-start | bytes 393224 | tf_op jit(solution)/shard_map/ppermute | solution.py:385
  53.7 0.7 copy-start
  54.3 0.7 copy-start.1
  67.3 0.7 copy-start.2
  87.3 22.5 %all-to-all-start.2 = ((bf16[16,96,128]{2,1,0:T(8,128)(2,1)}), bf16[16,96,128]{2,1,0:T(8,128)(2,1)S(1)}, u32[]{:S(2)}, u32[]{:S(2)}) async-start(bf16[16,96,128]{2,1,0:T(8,128)(2,1)} %window.1), calls=%async_computation.2 | async-start | bytes 786432 | tf_op jit(solution)/shard_map/all_to_all | solution.py:374
  112.5 12.1 %collective-permute-start.8 = (bf16[1536,128]{1,0:T(8,128)(2,1)S(1)}, bf16[1536,128]{1,0:T(8,128)(2,1)S(1)}, u32[]{:S(2)}, u32[]{:S(2)}) collective-permute-start(bf16[1536,128]{1,0:T(8,128)(2,1)S(1)} %project.3), channel_id=1, source_target_pairs={{0,1},{1,0},{2,3},{3,2},{4,5},{5,4},{6,7},{7,6},{8,9},{9,8},{10,11... | collective-permute-start | bytes 1179656 | tf_op jit(solution)/shard_map/ppermute | solution.py:449

commit v4 on v3

--- a/solution.py
+++ b/solution.py
@@ -37,88 +37,107 @@
             out_ref[p, base : base + rows, :] = piece
 
 
-def pack_query_kernel(head, q_ref, sk_ref, sv_ref, query_ref, sink_ref):
+def gather_facts(place, lengths, groups, need, blocks):
+    base = place[0] * RING * BLK
+    own = RING * BLK
+    for b in range((1 + G) * blocks):
+        need[b] = FAR
+    need[(1 + G) * blocks] = place[0]
+
+    def one_request(r, carry):
+        start, start_col, group_col = carry
+        length = lengths[r]
+        group = groups[r]
+        first = jnp.where(start < base, 0, (start - base) // QB)
+        last = jnp.minimum((start + length - 1 - base) // QB, blocks - 1)
+
+        def mark(b, _):
+            need[b] = jnp.minimum(need[b], start)
+            offset = jnp.maximum(base + b * QB - start, 0)
+            at = (1 + group) * blocks + b
+            need[at] = jnp.minimum(need[at], offset)
+            return 0
+
+        @pl.when((start < base + own) & (start + length > base))
+        def _():
+            lax.fori_loop(first, last + 1, mark, 0)
+
+        row = lax.broadcasted_iota(jnp.int32, start_col.shape, 0)
+        start_col = jnp.where(row == r, start, start_col)
+        group_col = jnp.where(row == r, group, group_col)
+        return (start + length, start_col, group_col)
+
+    reqs = lengths.shape[0]
+    column = jnp.zeros((reqs, QB), jnp.int32)
+    _, start_col, group_col = lax.fori_loop(0, reqs, one_request, (jnp.int32(0), column, column))
+    return base, start_col, group_col
+
+
+def query_facts(index, start_col, group_col):
+    begun = start_col <= index
+    start_q = jnp.max(jnp.where(begun, start_col, 0), axis=0, keepdims=True)
+    here = begun & (start_col == start_q)
+    group_q = jnp.max(jnp.where(here, group_col, 0), axis=0, keepdims=True)
+    return jnp.maximum(start_q, index - (W - 1)), index - start_q, group_q
+
+
+def turn(piece):
+    pad = jnp.zeros((LANES - HD, BLK), jnp.bfloat16)
+    return jnp.concatenate([piece, pad], axis=0).T
+
+
+def query_block(query_ref, b):
+    q_t = jnp.concatenate([query_ref[2 * b], query_ref[2 * b + 1]], axis=1)
+    scaled = q_t.astype(jnp.float32) * FACTOR
+    high = scaled.astype(jnp.bfloat16)
+    low = (scaled - high.astype(jnp.float32)).astype(jnp.bfloat16)
+    pad = jnp.zeros((LANES - HD, QB), jnp.bfloat16)
+    return jnp.concatenate([high, pad, low, pad], axis=0)
+
+
+def score(keys, q_t):
+    return dot(jnp.concatenate([keys, keys], axis=1), q_t)
+
+
+def values(val_ref, at):
+    slot = at // BLK
+    return jnp.concatenate([val_ref[slot], val_ref[slot + 1]], axis=1)
+
+
+def dot(a, b):
+    return jnp.dot(a, b, preferred_element_type=jnp.float32)
+
+
+FACTOR = (1.0 / math.sqrt(HD)) * math.log2(math.e)
+
+
+def prep_kernel(
+    need_in, sink_in, low_in, own_ref, key_ref, need, sink_ref, low_ref, last_ref
+):
+    for j in range(RING // 2):
+        last_ref[j] = own_ref[RING // 2 + j, 0 : 2 * HD, :]
+    sink_ref[...] = sink_in[...]
+    low_ref[...] = low_in[...]
+    for n in range(need.shape[0]):
+        need[n] = need_in[n]
+    for j in range(RING):
+        key_ref[j * BLK : (j + 1) * BLK, :] = turn(own_ref[j, 0:HD, :])
+
+
+def pack_query_kernel(
+    place, lengths, groups, q_ref, sk_ref, sv_ref, query_ref, sink_ref, low_ref, need
+):
     turned = q_ref[...].T
     for p in range(q_ref.shape[1] // HD):
         query_ref[p] = turned[p * HD : (p + 1) * HD, :]
     width = sk_ref.shape[1]
     column = lax.broadcasted_iota(jnp.int32, (width, LANES), 0)
     lane = lax.broadcasted_iota(jnp.int32, (width, LANES), 1)
-    pick = ((column == head[0] * HD + lane) & (lane < HD)).astype(jnp.float32).astype(jnp.bfloat16)
+    pick = ((column == place[1] * HD + lane) & (lane < HD)).astype(jnp.float32).astype(jnp.bfloat16)
     for which, ref in enumerate((sk_ref, sv_ref)):
         piece = jnp.dot(ref[...], pick, preferred_element_type=jnp.float32)
         piece = jnp.concatenate([piece, jnp.zeros_like(piece)], axis=0)
         sink_ref[which * 16 : (which + 1) * 16, :] = piece.astype(jnp.bfloat16)
-
-
-def gather_facts(place, lengths, groups, need, blocks):
-    base = place[0] * RING * BLK
-    own = RING * BLK
-    for b in range((1 + G) * blocks):
-        need[b] = FAR
-
-    def one_request(r, carry):
-        start, start_col, group_col = carry
-        length = lengths[r]
-        group = groups[r]
-        first = jnp.where(start < base, 0, (start - base) // QB)
-        last = jnp.minimum((start + length - 1 - base) // QB, blocks - 1)
-
-        def mark(b, _):
-            need[b] = jnp.minimum(need[b], start)
-            offset = jnp.maximum(base + b * QB - start, 0)
-            at = (1 + group) * blocks + b
-            need[at] = jnp.minimum(need[at], offset)
-            return 0
-
-        @pl.when((start < base + own) & (start + length > base))
-        def _():
-            lax.fori_loop(first, last + 1, mark, 0)
-
-        row = lax.broadcasted_iota(jnp.int32, start_col.shape, 0)
-        start_col = jnp.where(row == r, start, start_col)
-        group_col = jnp.where(row == r, group, group_col)
-        return (start + length, start_col, group_col)
-
-    reqs = lengths.shape[0]
-    column = jnp.zeros((reqs, QB), jnp.int32)
-    _, start_col, group_col = lax.fori_loop(0, reqs, one_request, (jnp.int32(0), column, column))
-    return base, start_col, group_col
-
-
-def query_facts(index, start_col, group_col):
-    begun = start_col <= index
-    start_q = jnp.max(jnp.where(begun, start_col, 0), axis=0, keepdims=True)
-    here = begun & (start_col == start_q)
-    group_q = jnp.max(jnp.where(here, group_col, 0), axis=0, keepdims=True)
-    return jnp.maximum(start_q, index - (W - 1)), index - start_q, group_q
-
-
-def turn(piece):
-    pad = jnp.zeros((LANES - HD, BLK), jnp.bfloat16)
-    return jnp.concatenate([piece, pad], axis=0).T
-
-
-def query_block(query_ref, b):
-    q_t = jnp.concatenate([query_ref[2 * b], query_ref[2 * b + 1]], axis=1)
-    return jnp.concatenate([q_t, jnp.zeros((LANES - HD, QB), jnp.bfloat16)], axis=0)
-
-
-def values(val_ref, at):
-    slot = at // BLK
-    return jnp.concatenate([val_ref[slot], val_ref[slot + 1]], axis=1)
-
-
-def dot(a, b):
-    return jnp.dot(a, b, preferred_element_type=jnp.float32)
-
-
-FACTOR = (1.0 / math.sqrt(HD)) * math.log2(math.e)
-
-
-def prep_kernel(place, lengths, groups, own_ref, key_ref, low_ref, need):
-    for j in range(RING):
-        key_ref[j * BLK : (j + 1) * BLK, :] = turn(own_ref[j, 0:HD, :])
     own = RING * BLK
     blocks = own // QB
     cache_at = own
@@ -136,6 +155,10 @@
         low_ref[b, 2 + G : 3 + G, :] = group_q
 
 
+def fold(rows, how):
+    return how(rows.reshape(rows.shape[0] // 8, 8, QB), axis=0)
+
+
 def visit(total, where_is, key_ref, val_ref, low_of, q_t, state):
     row_iota = lax.broadcasted_iota(jnp.int32, (CH, QB), 0)
 
@@ -144,19 +167,17 @@
         scores, ats = [], []
         for u in range(2):
             at, kind = where_is(2 * j + u)
-            s = dot(key_ref[pl.ds(at, CH), :], q_t)
+            s = score(key_ref[pl.ds(at, CH), :], q_t)
             scores.append(jnp.where(row_iota >= low_of(kind) - at, s, LOW))
             ats.append(at)
-        new = jnp.maximum(
-            jnp.max(scores[0], axis=0, keepdims=True), jnp.max(scores[1], axis=0, keepdims=True)
-        )
-        new = jnp.maximum(top, new)
-        fade = jnp.exp2((top - new) * FACTOR)
+        peak = jnp.maximum(fold(scores[0], jnp.max), fold(scores[1], jnp.max))
+        new = jnp.maximum(top, jnp.max(peak, axis=0, keepdims=True))
+        fade = jnp.exp2(top - new)
         den = den * fade
         ps = []
         for u in range(2):
-            p = jnp.exp2((scores[u] - new) * FACTOR)
-            den = den + jnp.sum(p, axis=0, keepdims=True)
+            p = jnp.exp2(scores[u] - new)
+            den = den + fold(p, jnp.sum)
             ps.append(p.astype(jnp.bfloat16))
         vals = jnp.concatenate([values(val_ref, at) for at in ats], axis=1)
         acc = acc * fade + dot(vals, jnp.concatenate(ps, axis=0))
@@ -166,14 +187,14 @@
 
 
 def attend_kernel(
-    place, need, low_ref, sink_ref, query_ref, own_ref, turned_ref, *rest, rings
+    need, low_ref, sink_ref, query_ref, own_ref, turned_ref, *rest, rings
 ):
     caches = rest[:rings]
     upper_ref, stat_ref, acc_ref, key_ref, val_ref = rest[rings:]
-    ring = place[0]
-    base = ring * RING * BLK
     own = RING * BLK
     blocks = own // QB
+    ring = need[(1 + G) * blocks]
+    base = ring * own
     key_ref[0:own, :] = turned_ref[...]
     for j in range(RING):
         val_ref[j] = own_ref[j, HD : 2 * HD, :]
@@ -196,14 +217,14 @@
         group_q = low_ref[b, 2 + G : 3 + G, :]
         q_t = query_block(query_ref, b)
         at0 = pl.multiple_of(b * QB, CH)
-        s_d = dot(key_ref[pl.ds(at0, CH), :], q_t)
+        s_d = score(key_ref[pl.ds(at0, CH), :], q_t)
         s_d = jnp.where((row_iota >= low_suffix - at0) & (row_iota <= lane), s_d, LOW)
-        s_s = dot(sink_ref[0:16, :], q_t)
+        s_s = score(sink_ref[0:16, :], q_t)
         s_s = jnp.where((sink_row // SINKS == group_q) & (sink_row < G * SINKS), s_s, LOW)
         top = jnp.maximum(jnp.max(s_d, axis=0, keepdims=True), jnp.max(s_s, axis=0, keepdims=True))
-        p_d = jnp.exp2((s_d - top) * FACTOR)
-        p_s = jnp.exp2((s_s - top) * FACTOR)
-        den = jnp.sum(p_d, axis=0, keepdims=True) + jnp.sum(p_s, axis=0, keepdims=True)
+        p_d = jnp.exp2(s_d - top)
+        p_s = jnp.exp2(s_s - top)
+        den = fold(p_d, jnp.sum) + fold(p_s, jnp.sum)
         acc = dot(values(val_ref, at0), p_d.astype(jnp.bfloat16))
         acc = acc + dot(sink_v, p_s.astype(jnp.bfloat16))
 
@@ -231,17 +252,18 @@
         def low_of(kind):
             return low_ref[b, pl.ds(kind, 1), :]
 
-        top, den, acc = visit(total, where_is, key_ref, val_ref, low_of, q_t, (top, den, acc))
+        state = (top, den, acc)
+        top, den, acc = visit(total, where_is, key_ref, val_ref, low_of, q_t, state)
 
         @pl.when(b < blocks // 2)
         def _():
-            stat_ref[b, 0:1, :] = top
-            stat_ref[b, 1:2, :] = den
+            stat_ref[b, 0:8, :] = jnp.broadcast_to(top, (8, QB))
+            stat_ref[b, 8:16, :] = den
             acc_ref[b] = acc
 
         @pl.when(b >= blocks // 2)
         def _():
-            done = (acc / den).astype(jnp.bfloat16)
+            done = (acc / jnp.sum(den, axis=0, keepdims=True)).astype(jnp.bfloat16)
             upper_ref[2 * b - RING // 2] = done[:, 0:BLK]
             upper_ref[2 * b + 1 - RING // 2] = done[:, BLK:QB]
 
@@ -251,11 +273,11 @@
 
 
 def window_kernel(
-    place, need, low_ref, query_ref, win_ref, upper_ref, stat_ref, acc_ref, out_ref,
+    need, low_ref, query_ref, win_ref, upper_ref, stat_ref, acc_ref, out_ref,
     key_ref, val_ref,
 ):
-    base = place[0] * RING * BLK
     blocks = RING * BLK // QB
+    base = need[(1 + G) * blocks] * RING * BLK
     for j in range(RING // 2):
         key_ref[j * BLK : (j + 1) * BLK, :] = turn(win_ref[j, 0:HD, :])
         val_ref[j] = win_ref[j, HD : 2 * HD, :]
@@ -274,9 +296,9 @@
         def low_of(kind):
             return low_ref[b, pl.ds(kind, 1), :] + jnp.where(kind == 0, W, 0)
 
-        state = (stat_ref[b, 0:1, :], stat_ref[b, 1:2, :], acc_ref[b])
+        state = (stat_ref[b, 0:1, :], stat_ref[b, 8:16, :], acc_ref[b])
         _, den, acc = visit(total, where_is, key_ref, val_ref, low_of, q_t, state)
-        done = (acc / den).astype(jnp.bfloat16)
+        done = (acc / jnp.sum(den, axis=0, keepdims=True)).astype(jnp.bfloat16)
         out_ref[2 * b] = done[:, 0:BLK]
         out_ref[2 * b + 1] = done[:, BLK:QB]
         return 0
@@ -357,17 +379,22 @@
         out_specs=vmem(),
         name="pack",
     )(keys, values, cache_k, cache_v)
-    packed_q, sinks = pl.pallas_call(
+    own = RING * BLK
+    blocks = own // QB
+    place = jnp.stack([device // RING, device % RING]).astype(jnp.int32)
+    packed_q, sinks, lows, need = pl.pallas_call(
         pack_query_kernel,
         out_shape=(
             jax.ShapeDtypeStruct((heads, HD, LANES), jnp.bfloat16),
             jax.ShapeDtypeStruct((32, LANES), jnp.bfloat16),
-        ),
-        in_specs=[smem()] + [vmem()] * 3,
-        out_specs=(vmem(), vmem()),
+            jax.ShapeDtypeStruct((blocks, 8, QB), jnp.int32),
+            jax.ShapeDtypeStruct(((1 + G) * blocks + 1,), jnp.int32),
+        ),
+        in_specs=[smem()] * 3 + [vmem()] * 3,
+        out_specs=(vmem(), vmem(), vmem(), smem()),
         cost_estimate=pl.CostEstimate(flops=1 << 20, bytes_accessed=1 << 21, transcendentals=0),
         name="pack_query",
-    )((device % RING).reshape(1), queries, sink_k, sink_v)
+    )(place, suffix_lengths, request_group, queries, sink_k, sink_v)
     members = [[r * RING + i for i in range(RING)] for r in range(rings)]
 
     def trade(array, groups):
@@ -387,40 +414,37 @@
     near_y = send(cache, 0, 3)
     near_x = send(cache, 1, 0)
     back_y = send(cache, 0, 1)
-    far_y = send(near_y, 0, 3)
+    far_y = send(cache, 0, 2)
     near_xy = send(near_x, 0, 3)
     back_xy = send(back_y, 1, 0)
     far_xy = send(far_y, 1, 0)
-    window = lax.ppermute(
-        mine[RING // 2 :, : 2 * HD, :], "seq", [(s, s + RING) for s in range(seq - RING)]
-    )
     caches = [cache, near_y, far_y, back_y, near_x, near_xy, far_xy, back_xy]
-    own = RING * BLK
-    blocks = own // QB
-    place = (device // RING).reshape(1)
-    turned, lows, need = pl.pallas_call(
+    turned, need, sinks, lows, last = pl.pallas_call(
         prep_kernel,
         out_shape=(
             jax.ShapeDtypeStruct((own, LANES), jnp.bfloat16),
-            jax.ShapeDtypeStruct((blocks, 8, QB), jnp.int32),
-            jax.ShapeDtypeStruct(((1 + G) * blocks,), jnp.int32),
-        ),
-        in_specs=[smem()] * 3 + [vmem()],
-        out_specs=(vmem(), vmem(), smem()),
+            jax.ShapeDtypeStruct(need.shape, need.dtype),
+            jax.ShapeDtypeStruct(sinks.shape, sinks.dtype),
+            jax.ShapeDtypeStruct(lows.shape, lows.dtype),
+            jax.ShapeDtypeStruct((RING // 2, 2 * HD, LANES), jnp.bfloat16),
+        ),
+        in_specs=[smem()] + [vmem()] * 3,
+        out_specs=(vmem(), smem(), vmem(), vmem(), vmem()),
         cost_estimate=pl.CostEstimate(
             flops=1 << 20, bytes_accessed=1 << 22, transcendentals=0
         ),
         compiler_params=pltpu.CompilerParams(vmem_limit_bytes=VMEM_LIMIT),
         name="prep",
-    )(place, suffix_lengths, request_group, mine)
+    )(need, sinks, lows, mine)
+    window = lax.ppermute(last, "seq", [(s, s + RING) for s in range(seq - RING)])
     upper, stats, sums = pl.pallas_call(
         functools.partial(attend_kernel, rings=rings),
         out_shape=(
             jax.ShapeDtypeStruct((RING // 2, HD, BLK), jnp.bfloat16),
-            jax.ShapeDtypeStruct((blocks // 2, 8, QB), jnp.float32),
+            jax.ShapeDtypeStruct((blocks // 2, 16, QB), jnp.float32),
             jax.ShapeDtypeStruct((blocks // 2, HD, QB), jnp.float32),
         ),
-        in_specs=[smem()] * 2 + [vmem()] * (5 + rings),
+        in_specs=[smem()] + [vmem()] * (5 + rings),
         out_specs=(vmem(), vmem(), vmem()),
         scratch_shapes=[
             pltpu.VMEM((own + G * W, LANES), jnp.bfloat16),
@@ -431,11 +455,11 @@
         ),
         compiler_params=pltpu.CompilerParams(vmem_limit_bytes=VMEM_LIMIT),
         name="attend",
-    )(place, need, lows, sinks, mine_q, mine, turned, *caches)
+    )(need, lows, sinks, mine_q, mine, turned, *caches)
     attn = pl.pallas_call(
         window_kernel,
         out_shape=jax.ShapeDtypeStruct((RING, HD, BLK), jnp.bfloat16),
-        in_specs=[smem()] * 2 + [vmem()] * 6,
+        in_specs=[smem()] + [vmem()] * 6,
         out_specs=vmem(),
         scratch_shapes=[
             pltpu.VMEM((W, LANES), jnp.bfloat16),
@@ -443,7 +467,7 @@
         ],
         compiler_params=pltpu.CompilerParams(vmem_limit_bytes=VMEM_LIMIT),
         name="window",
-    )(place, need, lows, mine_q, window, upper, stats, sums)
+    )(need, lows, mine_q, window, upper, stats, sums)
     attn_t = trade(attn, members).reshape(width, rows)
     give = project(1 - half, attn_t, w_out, jnp.bfloat16)
     got = lax.ppermute(give, "head", [(0, 1), (1, 0)])

time: 126 us -> 124 us (0.984)
  the two profiles are of different devices: /device:TPU:27 before, /device:TPU:31 now
where the time goes in v4:
time: 124 us; the launch traced here: 123 us
  waiting for transfers between devices  57.3 us (46%)
  Pallas kernels  31.9 us (26%)
  starting transfers between devices  30.3 us (24%)
  local copies, waits for them, and re-layouts  2.15 us (2%)
  other arithmetic  1.5 us (1%)
    all_to_all x3, waiting for transfers between devices, trade(): lax.all_to_all(array, 'seq', 0, 0, axis_index_groups=groups, tiled=True)  38.7 us
    all_to_all x3, starting transfers between devices, trade(): lax.all_to_all(array, 'seq', 0, 0, axis_index_groups=groups, tiled=True)  20.8 us
    pallas_call x1, Pallas kernels, shards(): pl.pallas_call(functools.partial(attend_kernel, rings=rings), out_shape=(...  17.4 us
    ppermute x7, waiting for transfers between devices, send(): return lax.ppermute(array, 'seq', pairs)  10.3 us
    ppermute x1, waiting for transfers between devices, shards(): got = lax.ppermute(give, 'head', [(0, 1), (1, 0)])  8.39 us
    ppermute x7, starting transfers between devices, send(): return lax.ppermute(array, 'seq', pairs)  7.22 us
    pallas_call x2, Pallas kernels, project(): pl.pallas_call(project_kernel, out_shape=jax.ShapeDtypeStruct((features,...  5.54 us
    pallas_call x1, Pallas kernels, shards(): pl.pallas_call(pack_query_kernel, out_shape=(jax.ShapeDtypeStruct((heads,...  2.88 us
  transfers between devices with their start and end apart: 12, of which 7 were waited for; matrix products, arithmetic and copies ran while one was open for 1% of the time, Pallas kernels for 20%

profile of v4, /device:TPU:31, one launch (start us, length us, event | category | flops | bytes accessed | tf_op | source)
XLA Modules:
  0.0 123.2 jit_solution(2380165864335235679)
XLA Ops:
  0.0 2.4 %pack.1 = bf16[16,224,128]{2,1,0:T(8,128)(2,1)} custom-call(bf16[128,1536]{1,0:T(8,128)(2,1)} %k_ref.1, bf16[128,1536]{1,0:T(8,128)(2,1)} %v_ref.1, bf16[16,1536]{1,0:T(8,128)(2,1)} %ck_ref.1, bf16[16,1536]{1,0:T(8,128)(2,1)} %cv_ref.1), custom_call_target="tpu_custom_call" | custom-call | tf_op jit(solution)/shard_map/pack/pallas_call | solution.py:375
  2.4 9.2 %all-to-all-start = ((bf16[16,224,128]{2,1,0:T(8,128)(2,1)}), bf16[16,224,128]{2,1,0:T(8,128)(2,1)S(1)}, u32[]{:S(2)}, u32[]{:S(2)}) async-start(bf16[16,224,128]{2,1,0:T(8,128)(2,1)} %pack.1), calls=%async_computation | async-start | bytes 1835008 | tf_op jit(solution)/shard_map/all_to_all | solution.py:401
  11.5 0.7 pad_add_fusion.place
  12.2 2.9 %pack_query.1 = (bf16[16,96,128]{2,1,0:T(8,128)(2,1)}, bf16[32,128]{1,0:T(8,128)(2,1)}, s32[8,8,256]{2,1,0:T(8,128)}, s32[25]{0:T(128)}) custom-call(s32[2]{0:T(128)} %pad_add_fusion.place, s32[32]{0:T(128)} %lengths.1, s32[32]{0:T(128)} %groups.1, bf16[128,1536]{1,0:T(8,128)(2,1)} %q_ref.1, bf16[8,1536]{1,0:T(8,128)(2,1)} %sk_ref.1, bf16[8,1536]{1,0:T(8,128)(2,1)} %sv_ref.1), custom_call_target="tpu_custom_call" | custom-call | flops 1048576 | bytes 2097152 | tf_op jit(solution)/shard_map/pack_query/pallas_call | solution.py:385
  15.1 21.8 %all-to-all-done.own_ref = bf16[16,224,128]{2,1,0:T(8,128)(2,1)S(1)} async-done(((bf16[16,224,128]{2,1,0:T(8,128)(2,1)}), bf16[16,224,128]{2,1,0:T(8,128)(2,1)S(1)}, u32[]{:S(2)}, u32[]{:S(2)}) %all-to-all-start) | async-done | bytes 917536 | tf_op jit(solution)/shard_map/all_to_all | solution.py:401
  36.9 3.5 %all-to-all-start.1 = ((bf16[16,96,128]{2,1,0:T(8,128)(2,1)}), bf16[16,96,128]{2,1,0:T(8,128)(2,1)S(1)}, u32[]{:S(2)}, u32[]{:S(2)}) async-start(bf16[16,96,128]{2,1,0:T(8,128)(2,1)} %get-tuple-element.22), calls=%async_computation.1 | async-start | bytes 786432 | tf_op jit(solution)/shard_map/all_to_all | solution.py:401
  40.4 0.6 collective-permute-start.4
  41.0 1.0 collective-permute-start.2
  41.9 1.9 %collective-permute-start.3 = (bf16[16,32,128]{2,1,0:T(8,128)(2,1)S(1)}, bf16[16,32,128]{2,1,0:T(8,128)(2,1)S(1)}, u32[]{:S(2)}, u32[]{:S(2)}) collective-permute-start(bf16[16,32,128]{2,1,0:T(8,128)(2,1)S(1)} %slice.4.rest_0_), channel_id=1, source_target_pairs={{0,32},{2,34},{4,36},{6,38},{8,40},{10,42},{12,44},{14,46},{16,48}... | collective-permute-start | bytes 393224 | tf_op jit(solution)/shard_map/ppermute | solution.py:412
  43.9 0.8 copy-done
  44.7 0.7 copy-done.1
  45.4 0.6 copy-done.2
  46.0 1.1 prep.1
  47.2 1.3 %collective-permute-start = (bf16[8,192,128]{2,1,0:T(8,128)(2,1)S(1)}, bf16[8,192,128]{2,1,0:T(8,128)(2,1)S(1)}, u32[]{:S(2)}, u32[]{:S(2)}) collective-permute-start(bf16[8,192,128]{2,1,0:T(8,128)(2,1)S(1)} %get-tuple-element.23), channel_id=1, source_target_pairs={{0,32},{2,34},{4,36},{6,38},{8,40},{10,42},{12,44},{14,46},{16,48}... | collective-permute-start | bytes 1179656 | tf_op jit(solution)/shard_map/ppermute | solution.py:439
  48.5 2.2 %collective-permute-start.1 = (bf16[16,32,128]{2,1,0:T(8,128)(2,1)S(1)}, bf16[16,32,128]{2,1,0:T(8,128)(2,1)S(1)}, u32[]{:S(2)}, u32[]{:S(2)}) collective-permute-start(bf16[16,32,128]{2,1,0:T(8,128)(2,1)S(1)} %slice.4.rest_0_), channel_id=1, source_target_pairs={{0,96},{2,98},{4,100},{6,102},{8,104},{10,106},{12,108},{14,110},{... | collective-permute-start | bytes 393224 | tf_op jit(solution)/shard_map/ppermute | solution.py:412
  50.6 0.1 collective-permute-start.5
  50.7 0.9 collective-permute-start.6
  51.6 0.5 collective-permute-start.7
  52.2 2.3 %all-to-all-done.1.query_ref = bf16[16,96,128]{2,1,0:T(8,128)(2,1)S(1)} async-done(((bf16[16,96,128]{2,1,0:T(8,128)(2,1)}), bf16[16,96,128]{2,1,0:T(8,128)(2,1)S(1)}, u32[]{:S(2)}, u32[]{:S(2)}) %all-to-all-start.1) | async-done | bytes 393248 | tf_op jit(solution)/shard_map/all_to_all | solution.py:401
  54.5 2.5 %collective-permute-done.5.rest_5_ = bf16[16,32,128]{2,1,0:T(8,128)(2,1)S(1)} collective-permute-done((bf16[16,32,128]{2,1,0:T(8,128)(2,1)S(1)}, bf16[16,32,128]{2,1,0:T(8,128)(2,1)S(1)}, u32[]{:S(2)}, u32[]{:S(2)}) %collective-permute-start.5) | collective-permute-done | bytes 131104 | tf_op jit(solution)/shard_map/ppermute | solution.py:412
  57.0 5.0 %collective-permute-done.6.rest_6_ = bf16[16,32,128]{2,1,0:T(8,128)(2,1)} collective-permute-done((bf16[16,32,128]{2,1,0:T(8,128)(2,1)S(1)}, bf16[16,32,128]{2,1,0:T(8,128)(2,1)}, u32[]{:S(2)}, u32[]{:S(2)}) %collective-permute-start.6) | collective-permute-done | bytes 131104 | tf_op jit(solution)/shard_map/ppermute | solution.py:412
  62.0 2.8 %collective-permute-done.7.rest_7_ = bf16[16,32,128]{2,1,0:T(8,128)(2,1)} collective-permute-done((bf16[16,32,128]{2,1,0:T(8,128)(2,1)S(1)}, bf16[16,32,128]{2,1,0:T(8,128)(2,1)}, u32[]{:S(2)}, u32[]{:S(2)}) %collective-permute-start.7) | collective-permute-done | bytes 131104 | tf_op jit(solution)/shard_map/ppermute | solution.py:412
  64.8 17.4 %attend.1 = (bf16[8,96,128]{2,1,0:T(8,128)(2,1)S(1)}, f32[4,16,256]{2,1,0:T(8,128)S(1)}, f32[4,96,256]{2,1,0:T(8,128)S(1)}) custom-call(s32[25]{0:T(128)S(1)} %get-tuple-element.20.need, s32[8,8,256]{2,1,0:T(8,128)S(1)} %get-tuple-element.21.low_ref, bf16[32,128]{1,0:T(8,128)(2,1)S(1)} %get-tuple-element.24.sink_ref, ...), custom_call_target="tpu_custom_call" | custom-call | flops 1610612736 | bytes 4194304 | tf_op jit(solution)/shard_map/attend/pallas_call | solution.py:440
  82.2 0.0 collective-permute-done.win_ref
  82.3 2.5 %window.1 = bf16[16,96,128]{2,1,0:T(8,128)(2,1)} custom-call(s32[25]{0:T(128)S(1)} %get-tuple-element.20.need, s32[8,8,256]{2,1,0:T(8,128)S(1)} %get-tuple-element.21.low_ref, bf16[16,96,128]{2,1,0:T(8,128)(2,1)S(1)} %all-to-all-done.1.query_ref, bf16[8,192,128]{2,1,0:T(8,128)(2,1)S(1)} %collective-permute-done.win_ref, ...), custom_call_target="tpu_custom_call" | custom-call | tf_op jit(solution)/shard_map/window/pallas_call | solution.py:459
  84.8 8.2 %all-to-all-start.2 = ((bf16[16,96,128]{2,1,0:T(8,128)(2,1)}), bf16[16,96,128]{2,1,0:T(8,128)(2,1)S(1)}, u32[]{:S(2)}, u32[]{:S(2)}) async-start(bf16[16,96,128]{2,1,0:T(8,128)(2,1)} %window.1), calls=%async_computation.2 | async-start | bytes 786432 | tf_op jit(solution)/shard_map/all_to_all | solution.py:401
  93.0 14.5 %all-to-all-done.2 = bf16[16,96,128]{2,1,0:T(8,128)(2,1)S(1)} async-done(((bf16[16,96,128]{2,1,0:T(8,128)(2,1)}), bf16[16,96,128]{2,1,0:T(8,128)(2,1)S(1)}, u32[]{:S(2)}, u32[]{:S(2)}) %all-to-all-start.2) | async-done | bytes 393248 | tf_op jit(solution)/shard_map/all_to_all | solution.py:401
  107.5 2.7 %project.3 = bf16[1536,128]{1,0:T(8,128)(2,1)S(1)} custom-call(s32[1]{0:T(128)} %bitcast.4.side, bf16[1536,128]{1,0:T(8,128)(2,1)S(1)} %bitcast.5, bf16[1536,3072]{1,0:T(8,128)(2,1)} %w_ref.3), custom_call_target="tpu_custom_call" | custom-call | flops 603979776 | bytes 4718592 | tf_op jit(solution)/shard_map/project/pallas_call | solution.py:338
  110.3 0.9 collective-permute-start.8
  111.2 2.8 %project.2 = f32[1536,128]{1,0:T(8,128)S(1)} custom-call(s32[1]{0:T(128)} %bitcast.side, bf16[1536,128]{1,0:T(8,128)(2,1)S(1)} %bitcast.6, bf16[1536,3072]{1,0:T(8,128)(2,1)} %w_ref.3), custom_call_target="tpu_custom_call" | custom-call | flops 603979776 | bytes 4718592 | tf_op jit(solution)/shard_map/project/pallas_call | solution.py:338
  114.0 8.4 %collective-permute-done.8 = bf16[1536,128]{1,0:T(8,128)(2,1)S(1)} collective-permute-done((bf16[1536,128]{1,0:T(8,128)(2,1)S(1)}, bf16[1536,128]{1,0:T(8,128)(2,1)S(1)}, u32[]{:S(2)}, u32[]{:S(2)}) %collective-permute-start.8) | collective-permute-done | bytes 393248 | tf_op jit(solution)/shard_map/ppermute | solution.py:473
  122.4 0.8 add_convert_fusion
  (8 shorter events, 0.0 us)
Async XLA Ops:
  2.4 34.5 %all-to-all-start = ((bf16[16,224,128]{2,1,0:T(8,128)(2,1)}), bf16[16,224,128]{2,1,0:T(8,128)(2,1)S(1)}, u32[]{:S(2)}, u32[]{:S(2)}) async-start(bf16[16,224,128]{2,1,0:T(8,128)(2,1)} %pack.1), calls=%async_computation | async-start | bytes 1835008 | tf_op jit(solution)/shard_map/all_to_all | solution.py:401
  36.9 17.6 %all-to-all-start.1 = ((bf16[16,96,128]{2,1,0:T(8,128)(2,1)}), bf16[16,96,128]{2,1,0:T(8,128)(2,1)S(1)}, u32[]{:S(2)}, u32[]{:S(2)}) async-start(bf16[16,96,128]{2,1,0:T(8,128)(2,1)} %get-tuple-element.22), calls=%async_computation.1 | async-start | bytes 786432 | tf_op jit(solution)/shard_map/all_to_all | solution.py:401
  40.4 10.3 %collective-permute-start.4 = (bf16[16,32,128]{2,1,0:T(8,128)(2,1)S(1)}, bf16[16,32,128]{2,1,0:T(8,128)(2,1)S(1)}, u32[]{:S(2)}, u32[]{:S(2)}) collective-permute-start(bf16[16,32,128]{2,1,0:T(8,128)(2,1)S(1)} %slice.4.rest_0_), channel_id=1, source_target_pairs={{0,128},{2,130},{4,132},{6,134},{8,136},{10,138},{12,140},{14,142}... | collective-permute-start | bytes 393224 | tf_op jit(solution)/shard_map/ppermute | solution.py:412
  41.0 9.7 %collective-permute-start.2 = (bf16[16,32,128]{2,1,0:T(8,128)(2,1)S(1)}, bf16[16,32,128]{2,1,0:T(8,128)(2,1)S(1)}, u32[]{:S(2)}, u32[]{:S(2)}) collective-permute-start(bf16[16,32,128]{2,1,0:T(8,128)(2,1)S(1)} %slice.4.rest_0_), channel_id=1, source_target_pairs={{0,64},{2,66},{4,68},{6,70},{8,72},{10,74},{12,76},{14,78},{16,80}... | collective-permute-start | bytes 393224 | tf_op jit(solution)/shard_map/ppermute | solution.py:412
  41.9 9.7 %collective-permute-start.3 = (bf16[16,32,128]{2,1,0:T(8,128)(2,1)S(1)}, bf16[16,32,128]{2,1,0:T(8,128)(2,1)S(1)}, u32[]{:S(2)}, u32[]{:S(2)}) collective-permute-start(bf16[16,32,128]{2,1,0:T(8,128)(2,1)S(1)} %slice.4.rest_0_), channel_id=1, source_target_pairs={{0,32},{2,34},{4,36},{6,38},{8,40},{10,42},{12,44},{14,46},{16,48}... | collective-permute-start | bytes 393224 | tf_op jit(solution)/shard_map/ppermute | solution.py:412
  43.8 0.8 copy-start
  44.7 0.7 copy-start.1
  45.4 0.6 copy-start.2
  47.2 35.1 %collective-permute-start = (bf16[8,192,128]{2,1,0:T(8,128)(2,1)S(1)}, bf16[8,192,128]{2,1,0:T(8,128)(2,1)S(1)}, u32[]{:S(2)}, u32[]{:S(2)}) collective-permute-start(bf16[8,192,128]{2,1,0:T(8,128)(2,1)S(1)} %get-tuple-element.23), channel_id=1, source_target_pairs={{0,32},{2,34},{4,36},{6,38},{8,40},{10,42},{12,44},{14,46},{16,48}... | collective-permute-start | bytes 1179656 | tf_op jit(solution)/shard_map/ppermute | solution.py:439
  48.5 6.1 %collective-permute-start.1 = (bf16[16,32,128]{2,1,0:T(8,128)(2,1)S(1)}, bf16[16,32,128]{2,1,0:T(8,128)(2,1)S(1)}, u32[]{:S(2)}, u32[]{:S(2)}) collective-permute-start(bf16[16,32,128]{2,1,0:T(8,128)(2,1)S(1)} %slice.4.rest_0_), channel_id=1, source_target_pairs={{0,96},{2,98},{4,100},{6,102},{8,104},{10,106},{12,108},{14,110},{... | collective-permute-start | bytes 393224 | tf_op jit(solution)/shard_map/ppermute | solution.py:412
  50.6 6.4 %collective-permute-start.5 = (bf16[16,32,128]{2,1,0:T(8,128)(2,1)S(1)}, bf16[16,32,128]{2,1,0:T(8,128)(2,1)S(1)}, u32[]{:S(2)}, u32[]{:S(2)}) collective-permute-start(bf16[16,32,128]{2,1,0:T(8,128)(2,1)S(1)} %collective-permute-done.4.rest_4_), channel_id=1, source_target_pairs={{0,96},{2,98},{4,100},{6,102},{8,104},{10,106},{12,108},{14,110},{... | collective-permute-start | bytes 393224 | tf_op jit(solution)/shard_map/ppermute | solution.py:412
  50.7 11.3 %collective-permute-start.6 = (bf16[16,32,128]{2,1,0:T(8,128)(2,1)S(1)}, bf16[16,32,128]{2,1,0:T(8,128)(2,1)}, u32[]{:S(2)}, u32[]{:S(2)}) collective-permute-start(bf16[16,32,128]{2,1,0:T(8,128)(2,1)S(1)} %collective-permute-done.2.rest_2_), channel_id=1, source_target_pairs={{0,128},{2,130},{4,132},{6,134},{8,136},{10,138},{12,140},{14,142}... | collective-permute-start | bytes 393224 | tf_op jit(solution)/shard_map/ppermute | solution.py:412
  51.6 13.2 %collective-permute-start.7 = (bf16[16,32,128]{2,1,0:T(8,128)(2,1)S(1)}, bf16[16,32,128]{2,1,0:T(8,128)(2,1)}, u32[]{:S(2)}, u32[]{:S(2)}) collective-permute-start(bf16[16,32,128]{2,1,0:T(8,128)(2,1)S(1)} %collective-permute-done.3.rest_3_), channel_id=1, source_target_pairs={{0,128},{2,130},{4,132},{6,134},{8,136},{10,138},{12,140},{14,142}... | collective-permute-start | bytes 393224 | tf_op jit(solution)/shard_map/ppermute | solution.py:412
  84.8 22.7 %all-to-all-start.2 = ((bf16[16,96,128]{2,1,0:T(8,128)(2,1)}), bf16[16,96,128]{2,1,0:T(8,128)(2,1)S(1)}, u32[]{:S(2)}, u32[]{:S(2)}) async-start(bf16[16,96,128]{2,1,0:T(8,128)(2,1)} %window.1), calls=%async_computation.2 | async-start | bytes 786432 | tf_op jit(solution)/shard_map/all_to_all | solution.py:401
  110.3 12.1 %collective-permute-start.8 = (bf16[1536,128]{1,0:T(8,128)(2,1)S(1)}, bf16[1536,128]{1,0:T(8,128)(2,1)S(1)}, u32[]{:S(2)}, u32[]{:S(2)}) collective-permute-start(bf16[1536,128]{1,0:T(8,128)(2,1)S(1)} %project.3), channel_id=1, source_target_pairs={{0,1},{1,0},{2,3},{3,2},{4,5},{5,4},{6,7},{7,6},{8,9},{9,8},{10,11... | collective-permute-start | bytes 1179656 | tf_op jit(solution)/shard_map/ppermute | solution.py:473
